TPU v7x, 32 devices: a whole 2x2x4 slice. The times are simulated.
32 devices in a mesh: gx: 2 (over y), gy: 4 (over z), gz: 4 (over x, core).
Axes of the slice: x: 2, y: 2, z: 4, core: 2. Of those that a mesh axis runs over, the one named last changes fastest.
Arguments:
- positions: float32 [4, 4, 4, 3, 32], P('gx', 'gy', 'gz'), may hold values from 0 to 5, as said below
- counts: int32 [4, 4, 4], P('gx', 'gy', 'gz'), may hold values from 1 to 32, as said below
- scalars: bfloat16 [4, 4, 4, 32, 128], P('gx', 'gy', 'gz'), may hold values from -6 to 6
- vectors: bfloat16 [4, 4, 4, 32, 3, 128], P('gx', 'gy', 'gz'), may hold values from -6 to 6
- radial_in: bfloat16 [2, 8, 64], replicated, may hold values from -2 to 2
- radial_bias: float32 [2, 64], replicated, may hold values from -3 to 3
- radial_out: bfloat16 [2, 64, 512], replicated, may hold values from -0.75 to 0.75
- atom_in: bfloat16 [2, 128, 128], replicated, may hold values from -0.5 to 0.5
- atom_bias: float32 [2, 128], replicated, may hold values from -3 to 3
- atom_out: bfloat16 [2, 128, 512], replicated, may hold values from -0.5 to 0.5
- readout_in: bfloat16 [128, 64], replicated, may hold values from -0.5 to 0.5
- readout_out: float32 [64], replicated, may hold values from -0.75 to 0.75
Outputs:
- scalars_out: bfloat16 [4, 4, 4, 32, 128], P('gx', 'gy', 'gz')
- vectors_out: bfloat16 [4, 4, 4, 32, 3, 128], P('gx', 'gy', 'gz')
- energy: float32 [1], replicated
Inputs may be any that keep to these rules, and one draw needn't show every extreme that they name: `counts`: some cell of every draw holds 32 atoms and some other cell one atom. `positions`: the slots of a cell sit on distinct sites of a jittered lattice, so that any two slots, also of neighbouring cells, lie at least 0.5 apart.
All inputs are finite; a program needn't handle non-finite values.
Results may differ from a plain program's by a relative error of at most 0.0075.
Values may be sent and summed in bfloat16 or wider, within the bound.
A program may use at most 64 MiB of HBM per device.

v0:
```python
import math

import jax
import jax.numpy as jnp
from jax import lax
from jax.sharding import PartitionSpec as P

cutoff = 5.0
message_scale = 0.5


def extended(block, sides, width):
    for axis, dim in sides:
        count = lax.axis_size(axis)
        forward = [(i, i + 1) for i in range(count - 1)]
        forward.append((count - 1, 0))
        backward = [(target, source) for source, target in forward]
        low = lax.ppermute(
            lax.slice_in_dim(block, block.shape[dim] - width, None, axis=dim), axis, forward
        )
        high = lax.ppermute(lax.slice_in_dim(block, 0, width, axis=dim), axis, backward)
        block = jnp.concatenate([low, block, high], axis=dim)
    return block


def offsets_table():
    index = lax.broadcasted_iota(jnp.int32, (27, 3), 0)
    column = lax.broadcasted_iota(jnp.int32, (27, 3), 1)
    digit = jnp.where(column == 0, index // 9, jnp.where(column == 1, index // 3 % 3, index % 3))
    return (digit - 1).astype(jnp.float32)


def atom_gates(states, atom_in, atom_bias, atom_out):
    lead = states.shape[:-1]
    width = states.shape[-1]
    flat = states.reshape(-1, width)
    hidden = jax.nn.silu(
        jnp.dot(flat, atom_in, preferred_element_type=jnp.float32) + atom_bias
    ).astype(jnp.bfloat16)
    gates = jnp.dot(hidden, atom_out, preferred_element_type=jnp.float32).astype(jnp.bfloat16)
    return gates.reshape(lead + (4, width))


def receiver_block(
    start,
    row_count,
    near_pos,
    near_live,
    own_pos,
    plain_side,
    gate_c,
    pair_g,
    radial_in,
    radial_bias,
    radial_out,
):
    slots = own_pos.shape[1]
    near_count = near_pos.shape[0]
    width = gate_c.shape[-1]
    mine = lax.dynamic_slice_in_dim(own_pos, start, row_count, 1).T
    displace = near_pos[None, :, :] - mine[:, None, :]
    row_index = start + lax.broadcasted_iota(jnp.int32, (row_count, near_count), 0)
    col_index = lax.broadcasted_iota(jnp.int32, (row_count, near_count), 1)
    itself = (col_index == row_index + 13 * slots).astype(jnp.float32)
    distance = jnp.sqrt(jnp.sum(displace * displace, axis=-1) + itself)
    unit = displace / distance[:, :, None]
    smooth = jnp.where(distance < cutoff, 0.5 * (jnp.cos(math.pi * distance / cutoff) + 1.0), 0.0)
    weight = smooth * near_live[None, :] * (1.0 - itself)
    basis_count = radial_in.shape[0]
    centers = lax.broadcasted_iota(jnp.float32, (basis_count,), 0) * (cutoff / (basis_count - 1))
    sharpness = 0.5 * ((basis_count - 1) / cutoff) ** 2
    basis = jnp.exp(-sharpness * (distance[:, :, None] - centers) ** 2).astype(jnp.bfloat16)
    hidden = (
        jnp.dot(basis.reshape(-1, basis_count), radial_in, preferred_element_type=jnp.float32)
        + radial_bias
    )
    hidden = jax.nn.silu(hidden).reshape(row_count, near_count, -1) * weight[:, :, None]
    edge = jnp.concatenate(
        [hidden[:, :, None, :], hidden[:, :, None, :] * unit[:, :, :, None]], axis=2
    ).astype(jnp.bfloat16)
    edge_plain = edge[:, :, 0, :]
    edge_turned = edge[:, :, 1:, :]
    scalar_part = lax.dot_general(
        edge_plain, plain_side, (((1,), (0,)), ((), ())), preferred_element_type=jnp.float32
    )
    along_part = lax.dot_general(
        edge_turned, gate_c, (((1,), (0,)), ((), ())), preferred_element_type=jnp.float32
    )
    project_part = lax.dot_general(
        edge_turned, pair_g, (((1, 2), (0, 1)), ((), ())), preferred_element_type=jnp.float32
    )
    filters = radial_out.astype(jnp.float32).reshape(-1, 4, width)
    term_a = scalar_part[:, :, :width]
    term_b = scalar_part[:, :, width:].reshape(row_count, -1, 3, width)
    scalar_delta = message_scale * (
        jnp.sum(term_a * filters[None, :, 0, :], axis=1)
        + jnp.sum(project_part * filters[None, :, 3, :], axis=1)
    )
    vector_delta = message_scale * (
        jnp.sum(term_b * filters[None, :, None, 1, :], axis=1)
        + jnp.sum(along_part * filters[None, None, :, 2, :], axis=2)
    )
    return (scalar_delta, vector_delta)


def cell_deltas(cell, geo_pad, feat_pad, layer_params):
    radial_in, radial_bias, radial_out, atom_in, atom_bias, atom_out = layer_params
    cells_deep = geo_pad.shape[1] - 2
    cells_tall = geo_pad.shape[2] - 2
    slots = geo_pad.shape[4]
    width = feat_pad.shape[-1]
    at_x = cell // (cells_deep * cells_tall)
    at_y = cell // cells_tall % cells_deep
    at_z = cell % cells_tall
    zero = jnp.zeros((), jnp.int32)
    geo_near = lax.dynamic_slice(
        geo_pad, (at_x, at_y, at_z, zero, zero), (3, 3, 3) + geo_pad.shape[3:]
    ).reshape((27,) + geo_pad.shape[3:])
    feat_near = lax.dynamic_slice(
        feat_pad, (at_x, at_y, at_z, zero, zero, zero), (3, 3, 3) + feat_pad.shape[3:]
    ).reshape((27 * slots,) + feat_pad.shape[4:])
    near_pos = (
        (geo_near[:, :3, :] + offsets_table()[:, :, None] * cutoff)
        .transpose(0, 2, 1)
        .reshape(27 * slots, 3)
    )
    near_live = geo_near[:, 3, :].reshape(27 * slots)
    own_pos = geo_near[13, :3, :]
    gates = feat_near[:, :4, :]
    near_vectors = feat_near[:, 4:, :].astype(jnp.float32)
    pair_b = (gates[:, 1, None, :].astype(jnp.float32) * near_vectors).astype(jnp.bfloat16)
    pair_g = (gates[:, 3, None, :].astype(jnp.float32) * near_vectors).astype(jnp.bfloat16)
    plain_side = jnp.concatenate([gates[:, 0, :], pair_b.reshape(27 * slots, 3 * width)], axis=1)
    gate_c = gates[:, 2, :]
    row_count = slots // 8

    def compute_block(start):
        return receiver_block(
            start,
            row_count,
            near_pos,
            near_live,
            own_pos,
            plain_side,
            gate_c,
            pair_g,
            radial_in,
            radial_bias,
            radial_out,
        )

    def one_block(block):
        start = block * row_count
        return compute_block(start)

    scalar_delta, vector_delta = lax.map(one_block, jnp.arange(8, dtype=jnp.int32))
    return (scalar_delta.reshape(slots, width), vector_delta.reshape(slots, 3, width))


def all_deltas(geo_pad, feat_pad, layer_params, total_cells):

    def one_cell(cell):
        return cell_deltas(cell, geo_pad, feat_pad, layer_params)

    return lax.map(one_cell, jnp.arange(total_cells, dtype=jnp.int32))


def on_device(
    positions,
    counts,
    scalars,
    vectors,
    radial_in,
    radial_bias,
    radial_out,
    atom_in,
    atom_bias,
    atom_out,
    readout_in,
    readout_out,
):
    cells_wide, cells_deep, cells_tall, slots, width = scalars.shape
    total_cells = cells_wide * cells_deep * cells_tall
    live = (
        lax.broadcasted_iota(jnp.int32, (cells_wide, cells_deep, cells_tall, slots), 3)
        < counts[:, :, :, None]
    ).astype(jnp.float32)
    geometry = jnp.concatenate([positions, live[:, :, :, None, :]], axis=3)
    geo_pad = extended(geometry, (("gx", 0), ("gy", 1), ("gz", 2)), 1)
    scalar_state, vector_state = (scalars, vectors)
    for layer in range(radial_in.shape[0]):
        layer_params = (
            radial_in[layer],
            radial_bias[layer],
            radial_out[layer],
            atom_in[layer],
            atom_bias[layer],
            atom_out[layer],
        )
        own_gates = atom_gates(scalar_state, atom_in[layer], atom_bias[layer], atom_out[layer])
        stacked = jnp.concatenate([own_gates, vector_state], axis=4)
        feat_pad = extended(stacked, (("gx", 0), ("gy", 1), ("gz", 2)), 1)
        scalar_delta, vector_delta = all_deltas(geo_pad, feat_pad, layer_params, total_cells)
        scalar_delta = scalar_delta.reshape(cells_wide, cells_deep, cells_tall, slots, width)
        vector_delta = vector_delta.reshape(cells_wide, cells_deep, cells_tall, slots, 3, width)
        scalar_state = ((scalar_state.astype(jnp.float32) + scalar_delta) * live[..., None]).astype(
            jnp.bfloat16
        )
        vector_state = (
            (vector_state.astype(jnp.float32) + vector_delta) * live[..., None, None]
        ).astype(jnp.bfloat16)
    readout_hidden = jax.nn.silu(
        jnp.dot(scalar_state.reshape(-1, width), readout_in, preferred_element_type=jnp.float32)
    )
    atom_energy = jnp.sum(readout_hidden * readout_out, axis=-1) * live.reshape(-1)
    local_energy = jnp.sum(atom_energy)
    energy = lax.psum(local_energy, ("gx", "gy", "gz")).reshape(1)
    return (scalar_state, vector_state, energy)


def solution(mesh):
    in_specs = (
        P("gx", "gy", "gz", None, None),
        P("gx", "gy", "gz"),
        P("gx", "gy", "gz", None, None),
        P("gx", "gy", "gz", None, None, None),
        P(),
        P(),
        P(),
        P(),
        P(),
        P(),
        P(),
        P(),
    )
    out_specs = (P("gx", "gy", "gz", None, None), P("gx", "gy", "gz", None, None, None), P())
    return jax.shard_map(
        on_device, mesh=mesh, in_specs=in_specs, out_specs=out_specs, check_vma=False
    )
```

profile of v0, /device:TPU:0, one launch (start us, length us, event | category | flops | bytes accessed | tf_op | source)
XLA Modules:
  0.0 417.1 jit_solution(3915885405731303360)
XLA Ops:
  4.0 3.1 collective-permute-start.7
  8.6 2.0 collective-permute-start.1
  11.3 3.7 collective-permute-start.9
  17.8 3.2 collective-permute-done.9
  21.0 3.9 collective-permute-done.8
  25.6 1.8 collective-permute-start.3
  29.3 3.5 collective-permute-done.2
  34.0 6.4 %collective-permute-done.5 = f32[4,3,1,4,32]{4,3,2,1,0:T(4,128)S(1)} collective-permute-done((f32[4,3,1,4,32]{4,3,2,1,0:T(4,128)S(1)}, f32[4,3,1,4,32]{4,3,2,1,0:T(4,128)S(1)}, u32[]{:S(2)}, u32[]{:S(2)}) %collective-permute-start.5) | collective-permute-done | bytes 6176 | tf_op jit(solution)/shard_map/ppermute | solution.py:21
  40.4 2.9 collective-permute-done.4
  47.3 142.8 %while.87 = (s32[]{:T(128)}, f32[2,32,128]{2,1,0:T(8,128)}, f32[2,32,3,128]{3,1,2,0:T(8,128)}, s32[2]{0:T(128)}, f32[4,3,3,4,32]{4,3,2,1,0:T(4,128)}, /*index=5*...) while((s32[]{:T(128)}, f32[2,32,128]{2,1,0:T(8,128)}, ...), condition=%wide.region_8.9_spmd, body=%wide.region_0.8_spmd.sunk | while | flops 578568832 | bytes 32141488 | solution.py:165
  51.6 1.7 constant_dynamic-slice_fusion.15
  56.4 60.2 %while.90 = (s32[]{:T(128)}, f32[8,4,128]{2,1,0:T(4,128)S(1)}, f32[8,4,3,128]{3,2,1,0:T(4,128)}, f32[27,32,3]{1,0,2:T(8,128)}, s32[8]{0:T(128)S(1)}, /*index=5*/...) while((s32[]{:T(128)}, f32[8,4,128]{2,1,0:T(4,128)S(1)}, ...), condition=%wide.wide.region_7.7_spmd, body=%wide.wide.region_1.6_spmd.sunk | while | flops 574914944 | bytes 18360236 | solution.py:156
  123.0 1.7 constant_dynamic-slice_fusion.15
  127.8 60.2 %while.90 = (s32[]{:T(128)}, f32[8,4,128]{2,1,0:T(4,128)S(1)}, f32[8,4,3,128]{3,2,1,0:T(4,128)}, f32[27,32,3]{1,0,2:T(8,128)}, s32[8]{0:T(128)S(1)}, /*index=5*/...) while((s32[]{:T(128)}, f32[8,4,128]{2,1,0:T(4,128)S(1)}, ...), condition=%wide.wide.region_7.7_spmd, body=%wide.wide.region_1.6_spmd.sunk | while | flops 574914944 | bytes 18360236 | solution.py:156
  195.9 2.6 collective-permute-done.13
  199.1 1.8 collective-permute-start.15
  201.2 6.2 %collective-permute-done.15 = bf16[4,1,1,32,7,128]{5,3,2,1,0,4:T(8,128)(2,1)S(1)} collective-permute-done((bf16[4,1,1,32,7,128]{5,3,2,1,0,4:T(8,128)(2,1)S(1)}, bf16[4,1,1,32,7,128]{5,3,2,1,0,4:T(8,128)(2,1)S(1)}, u32[]{:S(2)}, u32[]{:S(2)}) %collective-permute-start.15) | collective-permute-done | bytes 229408 | tf_op jit(solution)/shard_map/ppermute | solution.py:21
  207.5 3.8 collective-permute-done.14
  213.3 13.8 %collective-permute-done.17 = bf16[4,3,1,32,7,128]{5,3,2,1,0,4:T(8,128)(2,1)S(1)} collective-permute-done((bf16[4,3,1,32,7,128]{5,3,2,1,0,4:T(8,128)(2,1)S(1)}, bf16[4,3,1,32,7,128]{5,3,2,1,0,4:T(8,128)(2,1)S(1)}, u32[]{:S(2)}, u32[]{:S(2)}) %collective-permute-start.17) | collective-permute-done | bytes 688160 | tf_op jit(solution)/shard_map/ppermute | solution.py:21
  230.9 140.5 %while.89 = (s32[]{:T(128)}, f32[2,32,128]{2,1,0:T(8,128)}, f32[2,32,3,128]{3,1,2,0:T(8,128)}, s32[2]{0:T(128)}, f32[4,3,3,4,32]{4,3,2,1,0:T(4,128)}, /*index=5*...) while((s32[]{:T(128)}, f32[2,32,128]{2,1,0:T(8,128)}, ...), condition=%wide.region_17.18_spmd, body=%wide.region_9.17_spmd.sunk | while | flops 578568832 | bytes 32139408 | solution.py:165
  235.3 1.7 constant_dynamic-slice_fusion.17
  240.1 59.1 %while.91 = (s32[]{:T(128)}, f32[8,4,128]{2,1,0:T(4,128)S(1)}, f32[8,4,3,128]{3,2,1,0:T(4,128)}, f32[27,32,3]{1,0,2:T(8,128)}, s32[8]{0:T(128)S(1)}, /*index=5*/...) while((s32[]{:T(128)}, f32[8,4,128]{2,1,0:T(4,128)S(1)}, ...), condition=%wide.wide.region_16.16_spmd, body=%wide.wide.region_10.15_spmd.sunk | while | flops 574914944 | bytes 18358132 | solution.py:156
  310.3 59.1 %while.91 = (s32[]{:T(128)}, f32[8,4,128]{2,1,0:T(4,128)S(1)}, f32[8,4,3,128]{3,2,1,0:T(4,128)}, f32[27,32,3]{1,0,2:T(8,128)}, s32[8]{0:T(128)S(1)}, /*index=5*/...) while((s32[]{:T(128)}, f32[8,4,128]{2,1,0:T(4,128)S(1)}, ...), condition=%wide.wide.region_16.16_spmd, body=%wide.wide.region_10.15_spmd.sunk | while | flops 574914944 | bytes 18358132 | solution.py:156
  376.0 41.1 %psum.7 = f32[1]{0:T(128)} all-reduce(f32[1]{0:T(128)} %bitcast.76), channel_id=1, replica_groups=mesh['gx'=2,'gy'=4,'gz'=4] {'gx','gy','gz'}, use_global_device_ids=true, to_apply=%region_20.21 | all-reduce | flops 1 | bytes 8 | tf_op jit(solution)/shard_map/psum | solution.py:217
  (1416 shorter events, 276.9 us)
Async XLA Ops:
  0.6 373.2 %copy-start = (bf16[128,64]{0,1:T(8,128)(2,1)S(1)}, bf16[128,64]{0,1:T(8,128)(2,1)}, u32[]{:S(2)}) copy-start(bf16[128,64]{0,1:T(8,128)(2,1)} %param.30) | copy-start | bytes 49156
  0.6 32.8 %copy-start.19 = (s32[2,1,1]{0,2,1:T(1,128)S(1)}, s32[2,1,1]{0,2,1:T(1,128)}, u32[]{:S(2)}) copy-start(s32[2,1,1]{0,2,1:T(1,128)} %param.21) | copy-start | bytes 28
  4.0 6.7 %collective-permute-start.7 = (bf16[1,1,1,32,7,128]{5,3,2,1,0,4:T(8,128)(2,1)S(1)}, bf16[1,1,1,32,7,128]{5,3,2,1,0,4:T(8,128)(2,1)S(1)}, u32[]{:S(2)}, u32[]{:S(2)}) collective-permute-start(bf16[1,1,1,32,7,128]{5,3,2,1,0,4:T(8,128)(2,1)S(1)} %get-tuple-element.994), channel_id=1, source_target_pairs={{16,0},{0,16},{17,1},{1,17},{18,2},{2,18},{19,3},{3,19},{20,4},{4,... | collective-permute-start | bytes 172040 | tf_op jit(solution)/shard_map/ppermute | solution.py:21
  7.1 4.2 %collective-permute-start.6 = (bf16[1,1,1,32,7,128]{5,3,2,1,0,4:T(8,128)(2,1)S(1)}, bf16[1,1,1,32,7,128]{5,3,2,1,0,4:T(8,128)(2,1)S(1)}, u32[]{:S(2)}, u32[]{:S(2)}) collective-permute-start(bf16[1,1,1,32,7,128]{5,3,2,1,0,4:T(8,128)(2,1)S(1)} %get-tuple-element.993), channel_id=1, source_target_pairs={{0,16},{16,0},{1,17},{17,1},{2,18},{18,2},{3,19},{19,3},{4,20},{20... | collective-permute-start | bytes 172040 | tf_op jit(solution)/shard_map/ppermute | solution.py:18
  8.6 17.0 %collective-permute-start.1 = (f32[1,1,1,4,32]{4,3,2,1,0:T(4,128)S(1)}, f32[1,1,1,4,32]{4,3,2,1,0:T(4,128)S(1)}, u32[]{:S(2)}, u32[]{:S(2)}) collective-permute-start(f32[1,1,1,4,32]{4,3,2,1,0:T(4,128)S(1)} %get-tuple-element.996), channel_id=1, source_target_pairs={{16,0},{0,16},{17,1},{1,17},{18,2},{2,18},{19,3},{3,19},{20,4},{4,... | collective-permute-start | bytes 1544 | tf_op jit(solution)/shard_map/ppermute | solution.py:21
  10.6 15.0 %collective-permute-start = (f32[1,1,1,4,32]{4,3,2,1,0:T(4,128)S(1)}, f32[1,1,1,4,32]{4,3,2,1,0:T(4,128)S(1)}, u32[]{:S(2)}, u32[]{:S(2)}) collective-permute-start(f32[1,1,1,4,32]{4,3,2,1,0:T(4,128)S(1)} %get-tuple-element.995), channel_id=1, source_target_pairs={{0,16},{16,0},{1,17},{17,1},{2,18},{18,2},{3,19},{19,3},{4,20},{20... | collective-permute-start | bytes 1544 | tf_op jit(solution)/shard_map/ppermute | solution.py:18
  11.3 9.6 %collective-permute-start.9 = (bf16[4,1,1,32,7,128]{5,3,2,1,0,4:T(8,128)(2,1)S(1)}, bf16[4,1,1,32,7,128]{5,3,2,1,0,4:T(8,128)(2,1)S(1)}, u32[]{:S(2)}, u32[]{:S(2)}) collective-permute-start(bf16[4,1,1,32,7,128]{5,3,2,1,0,4:T(8,128)(2,1)S(1)} %pad_maximum_fusion.6), channel_id=1, source_target_pairs={{4,0},{8,4},{12,8},{0,12},{5,1},{9,5},{13,9},{1,13},{6,2},{10,6},{... | collective-permute-start | bytes 688136 | tf_op jit(solution)/shard_map/ppermute | solution.py:21
  15.0 9.9 %collective-permute-start.8 = (bf16[4,1,1,32,7,128]{5,3,2,1,0,4:T(8,128)(2,1)S(1)}, bf16[4,1,1,32,7,128]{5,3,2,1,0,4:T(8,128)(2,1)S(1)}, u32[]{:S(2)}, u32[]{:S(2)}) collective-permute-start(bf16[4,1,1,32,7,128]{5,3,2,1,0,4:T(8,128)(2,1)S(1)} %pad_maximum_fusion.6), channel_id=1, source_target_pairs={{0,4},{4,8},{8,12},{12,0},{1,5},{5,9},{9,13},{13,1},{2,6},{6,10},{... | collective-permute-start | bytes 688136 | tf_op jit(solution)/shard_map/ppermute | solution.py:18
  25.0 19.0 %collective-permute-start.11 = (bf16[4,3,1,32,7,128]{5,3,2,1,0,4:T(8,128)(2,1)S(1)}, bf16[4,3,1,32,7,128]{5,3,2,1,0,4:T(8,128)(2,1)S(1)}, u32[]{:S(2)}, u32[]{:S(2)}) collective-permute-start(bf16[4,3,1,32,7,128]{5,3,2,1,0,4:T(8,128)(2,1)S(1)} %pad_maximum_fusion.4), channel_id=1, source_target_pairs={{1,0},{2,1},{3,2},{0,3},{5,4},{6,5},{7,6},{4,7},{9,8},{10,9},{11,1... | collective-permute-start | bytes 2064392 | tf_op jit(solution)/shard_map/ppermute | solution.py:21
  25.1 19.0 %collective-permute-start.10 = (bf16[4,3,1,32,7,128]{5,3,2,1,0,4:T(8,128)(2,1)S(1)}, bf16[4,3,1,32,7,128]{5,3,2,1,0,4:T(8,128)(2,1)S(1)}, u32[]{:S(2)}, u32[]{:S(2)}) collective-permute-start(bf16[4,3,1,32,7,128]{5,3,2,1,0,4:T(8,128)(2,1)S(1)} %pad_maximum_fusion.4), channel_id=1, source_target_pairs={{0,1},{1,2},{2,3},{3,0},{4,5},{5,6},{6,7},{7,4},{8,9},{9,10},{10,1... | collective-permute-start | bytes 2064392 | tf_op jit(solution)/shard_map/ppermute | solution.py:18
  25.6 3.7 collective-permute-start.3
  27.4 5.4 %collective-permute-start.2 = (f32[4,1,1,4,32]{4,3,2,1,0:T(4,128)S(1)}, f32[4,1,1,4,32]{4,3,2,1,0:T(4,128)S(1)}, u32[]{:S(2)}, u32[]{:S(2)}) collective-permute-start(f32[4,1,1,4,32]{4,3,2,1,0:T(4,128)S(1)} %pad_maximum_fusion.10), channel_id=1, source_target_pairs={{0,4},{4,8},{8,12},{12,0},{1,5},{5,9},{9,13},{13,1},{2,6},{6,10},{... | collective-permute-start | bytes 6152 | tf_op jit(solution)/shard_map/ppermute | solution.py:18
  32.9 7.6 %collective-permute-start.5 = (f32[4,3,1,4,32]{4,3,2,1,0:T(4,128)S(1)}, f32[4,3,1,4,32]{4,3,2,1,0:T(4,128)S(1)}, u32[]{:S(2)}, u32[]{:S(2)}) collective-permute-start(f32[4,3,1,4,32]{4,3,2,1,0:T(4,128)S(1)} %pad_maximum_fusion.9), channel_id=1, source_target_pairs={{1,0},{2,1},{3,2},{0,3},{5,4},{6,5},{7,6},{4,7},{9,8},{10,9},{11,1... | collective-permute-start | bytes 18440 | tf_op jit(solution)/shard_map/ppermute | solution.py:21
  32.9 10.4 %collective-permute-start.4 = (f32[4,3,1,4,32]{4,3,2,1,0:T(4,128)S(1)}, f32[4,3,1,4,32]{4,3,2,1,0:T(4,128)S(1)}, u32[]{:S(2)}, u32[]{:S(2)}) collective-permute-start(f32[4,3,1,4,32]{4,3,2,1,0:T(4,128)S(1)} %pad_maximum_fusion.9), channel_id=1, source_target_pairs={{0,1},{1,2},{2,3},{3,0},{4,5},{5,6},{6,7},{7,4},{8,9},{9,10},{10,1... | collective-permute-start | bytes 18440 | tf_op jit(solution)/shard_map/ppermute | solution.py:18
  47.3 142.8 %copy-start.10 = (f32[2,32]{1,0:T(2,128)S(1)}, f32[2,32]{1,0:T(2,128)}, u32[]{:S(2)}) copy-start(f32[2,32]{1,0:T(2,128)} %compare_convert_fusion.1) | copy-start | bytes 772
  47.3 144.3 %copy-start.16 = (f32[128]{0:T(128)S(1)}, f32[128]{0:T(128)}, u32[]{:S(2)}) copy-start(f32[128]{0:T(128)} %get-tuple-element.1001) | copy-start | bytes 1540
  193.8 4.7 %collective-permute-start.13 = (bf16[1,1,1,32,7,128]{5,3,2,1,0,4:T(8,128)(2,1)S(1)}, bf16[1,1,1,32,7,128]{5,3,2,1,0,4:T(8,128)(2,1)S(1)}, u32[]{:S(2)}, u32[]{:S(2)}) collective-permute-start(bf16[1,1,1,32,7,128]{5,3,2,1,0,4:T(8,128)(2,1)S(1)} %get-tuple-element.992), channel_id=1, source_target_pairs={{16,0},{0,16},{17,1},{1,17},{18,2},{2,18},{19,3},{3,19},{20,4},{4,... | collective-permute-start | bytes 172040 | tf_op jit(solution)/shard_map/ppermute | solution.py:21
  194.9 4.3 %collective-permute-start.12 = (bf16[1,1,1,32,7,128]{5,3,2,1,0,4:T(8,128)(2,1)S(1)}, bf16[1,1,1,32,7,128]{5,3,2,1,0,4:T(8,128)(2,1)S(1)}, u32[]{:S(2)}, u32[]{:S(2)}) collective-permute-start(bf16[1,1,1,32,7,128]{5,3,2,1,0,4:T(8,128)(2,1)S(1)} %get-tuple-element.991), channel_id=1, source_target_pairs={{0,16},{16,0},{1,17},{17,1},{2,18},{18,2},{3,19},{19,3},{4,20},{20... | collective-permute-start | bytes 172040 | tf_op jit(solution)/shard_map/ppermute | solution.py:18
  199.1 8.3 %collective-permute-start.15 = (bf16[4,1,1,32,7,128]{5,3,2,1,0,4:T(8,128)(2,1)S(1)}, bf16[4,1,1,32,7,128]{5,3,2,1,0,4:T(8,128)(2,1)S(1)}, u32[]{:S(2)}, u32[]{:S(2)}) collective-permute-start(bf16[4,1,1,32,7,128]{5,3,2,1,0,4:T(8,128)(2,1)S(1)} %pad_maximum_fusion.7), channel_id=1, source_target_pairs={{4,0},{8,4},{12,8},{0,12},{5,1},{9,5},{13,9},{1,13},{6,2},{10,6},{... | collective-permute-start | bytes 688136 | tf_op jit(solution)/shard_map/ppermute | solution.py:21
  201.0 10.3 %collective-permute-start.14 = (bf16[4,1,1,32,7,128]{5,3,2,1,0,4:T(8,128)(2,1)S(1)}, bf16[4,1,1,32,7,128]{5,3,2,1,0,4:T(8,128)(2,1)S(1)}, u32[]{:S(2)}, u32[]{:S(2)}) collective-permute-start(bf16[4,1,1,32,7,128]{5,3,2,1,0,4:T(8,128)(2,1)S(1)} %pad_maximum_fusion.7), channel_id=1, source_target_pairs={{0,4},{4,8},{8,12},{12,0},{1,5},{5,9},{9,13},{13,1},{2,6},{6,10},{... | collective-permute-start | bytes 688136 | tf_op jit(solution)/shard_map/ppermute | solution.py:18
  211.3 15.7 %collective-permute-start.17 = (bf16[4,3,1,32,7,128]{5,3,2,1,0,4:T(8,128)(2,1)S(1)}, bf16[4,3,1,32,7,128]{5,3,2,1,0,4:T(8,128)(2,1)S(1)}, u32[]{:S(2)}, u32[]{:S(2)}) collective-permute-start(bf16[4,3,1,32,7,128]{5,3,2,1,0,4:T(8,128)(2,1)S(1)} %pad_maximum_fusion.5), channel_id=1, source_target_pairs={{1,0},{2,1},{3,2},{0,3},{5,4},{6,5},{7,6},{4,7},{9,8},{10,9},{11,1... | collective-permute-start | bytes 2064392 | tf_op jit(solution)/shard_map/ppermute | solution.py:21
  211.4 16.3 %collective-permute-start.16 = (bf16[4,3,1,32,7,128]{5,3,2,1,0,4:T(8,128)(2,1)S(1)}, bf16[4,3,1,32,7,128]{5,3,2,1,0,4:T(8,128)(2,1)S(1)}, u32[]{:S(2)}, u32[]{:S(2)}) collective-permute-start(bf16[4,3,1,32,7,128]{5,3,2,1,0,4:T(8,128)(2,1)S(1)} %pad_maximum_fusion.5), channel_id=1, source_target_pairs={{0,1},{1,2},{2,3},{3,0},{4,5},{5,6},{6,7},{7,4},{8,9},{9,10},{10,1... | collective-permute-start | bytes 2064392 | tf_op jit(solution)/shard_map/ppermute | solution.py:18
  230.9 140.5 %copy-start.11 = (f32[2,32]{1,0:T(2,128)S(1)}, f32[2,32]{1,0:T(2,128)}, u32[]{:S(2)}) copy-start(f32[2,32]{1,0:T(2,128)} %compare_convert_fusion.1) | copy-start | bytes 772
  372.2 44.8 %copy-start.12 = (bf16[2,1,1,32,128]{4,3,2,1,0:T(8,128)(2,1)}, bf16[2,1,1,32,128]{4,3,2,1,0:T(8,128)(2,1)S(1)}, u32[]{:S(2)}) copy-start(bf16[2,1,1,32,128]{4,3,2,1,0:T(8,128)(2,1)S(1)} %fusion.95) | copy-start | bytes 49156
  (171 other events, 408.0 us)
where the time goes:
time: 419 us; the launch traced here: 417 us
  local copies, waits for them, and re-layouts  149 us (36%)
  matrix products  67.1 us (16%)
  other arithmetic  58.9 us (14%)
  waiting for transfers between devices  49.4 us (12%)
  blocking collectives  41.1 us (10%)
  loops' own time  34.5 us (8%)
  starting transfers between devices  16.8 us (4%)
    psum x1, blocking collectives, on_device(): energy = lax.psum(local_energy, ('gx', 'gy', 'gz')).reshape(1)  41.1 us
    reshape x64, local copies, waits for them, and re-layouts, receiver_block(): jax.nn.silu(hidden).reshape(row_count, near_count, -1) * weight[:, :, None]  40.2 us
    ppermute x9, waiting for transfers between devices, extended(): lax.ppermute(lax.slice_in_dim(block, 0, width, axis=dim), axis, backward)  33.3 us
    while x392, local copies, waits for them, and re-layouts  30.4 us
    another operation x4, loops' own time, cell_deltas(): lax.map(one_block, jnp.arange(8, dtype=jnp.int32))  26.3 us
    dynamic_slice x32, local copies, waits for them, and re-layouts, cell_deltas(): lax.map(one_block, jnp.arange(8, dtype=jnp.int32))  21 us
    dynamic_update_slice x64, other arithmetic, cell_deltas(): lax.map(one_block, jnp.arange(8, dtype=jnp.int32))  19.8 us
    dot_general x32, matrix products, receiver_block(): lax.dot_general(edge_turned, pair_g, (((1, 2), (0, 1)), ((), ())), prefer...  17.8 us
  transfers between devices with their start and end apart: 18, of which 13 were waited for; matrix products, arithmetic and copies ran while one was open for 2% of the time, Pallas kernels for 0%

commit v1 on v0

v1 whole, which is shorter than its diff:
```python
import functools
import math

import jax
import jax.numpy as jnp
from jax import lax
from jax.experimental import pallas as pl
from jax.experimental.pallas import tpu as pltpu
from jax.sharding import PartitionSpec as P

cutoff = 5.0
message_scale = 0.5
group = 8
chunk = 256


def extended(block, sides, width):
    for axis, dim in sides:
        count = lax.axis_size(axis)
        forward = [(i, i + 1) for i in range(count - 1)]
        forward.append((count - 1, 0))
        backward = [(target, source) for source, target in forward]
        low = lax.ppermute(
            lax.slice_in_dim(block, block.shape[dim] - width, None, axis=dim), axis, forward
        )
        high = lax.ppermute(lax.slice_in_dim(block, 0, width, axis=dim), axis, backward)
        block = jnp.concatenate([low, block, high], axis=dim)
    return block


def layer_kernel(
    grid_dims,
    max_chunks,
    counts,
    places,
    feats,
    radial_block,
    radial_bias,
    radial_out,
    atom_in,
    atom_bias,
    atom_out,
    out,
    near_place,
    near_state,
    place_rows,
    edges,
    plain_table,
    turned_table,
):
    deep, tall = grid_dims
    cell = pl.program_id(0)
    at_x = lax.div(cell, deep * tall)
    at_y = lax.rem(lax.div(cell, tall), deep)
    at_z = lax.rem(cell, tall)
    pad_y, pad_z = deep + 2, tall + 2
    slots = feats.shape[1]
    width = feats.shape[2] // 4
    hidden_width = radial_out.shape[0]
    basis_count = radial_block.shape[1] // group
    lane = lax.broadcasted_iota(jnp.int32, (slots, width), 1)

    def cell_index(dx, dy, dz):
        return ((at_x + dx) * pad_y + at_y + dy) * pad_z + at_z + dz

    home = cell_index(1, 1, 1)
    total = 0
    own_start = 0
    for dx in range(3):
        for dy in range(3):
            for dz in range(3):
                index = cell_index(dx, dy, dz)
                if (dx, dy, dz) == (1, 1, 1):
                    own_start = total
                shift = jnp.where(
                    lane == 0, float(dx - 1), jnp.where(lane == 1, float(dy - 1), float(dz - 1))
                )
                near_place[pl.ds(total, slots), :] = places[index] + shift * cutoff
                block = feats[index].astype(jnp.float32)
                for part in range(4):
                    near_state[part, pl.ds(total, slots), :] = block[
                        :, part * width : (part + 1) * width
                    ]
                total = total + counts[index]
    blank = jnp.zeros((chunk, width), jnp.float32)
    near_place[pl.ds(total, chunk), :] = blank
    for part in range(4):
        near_state[part, pl.ds(total, chunk), :] = blank
    chunks = lax.div(total + chunk - 1, chunk)

    @pl.loop(0, chunks)
    def _(step):
        rows = pl.ds(pl.multiple_of(step * chunk, chunk), chunk)
        place_rows[:, rows] = near_place[rows, :].T[:8, :]
        half = jnp.dot(
            near_state[0, rows, :].astype(jnp.bfloat16),
            atom_in[...],
            preferred_element_type=jnp.float32,
        ) + atom_bias[...]
        hidden = (half + half * jnp.tanh(half)).astype(jnp.bfloat16)
        gates = jnp.dot(hidden, atom_out[...], preferred_element_type=jnp.float32).astype(
            jnp.bfloat16
        )
        plain_table[rows, :width] = gates[:, :width]
        gate_b = gates[:, width : 2 * width].astype(jnp.float32)
        gate_c = gates[:, 2 * width : 3 * width]
        gate_g = gates[:, 3 * width :].astype(jnp.float32)
        for part in range(3):
            vector = near_state[part + 1, rows, :]
            plain_table[rows, (part + 1) * width : (part + 2) * width] = (gate_b * vector).astype(
                jnp.bfloat16
            )
            turned_table[part, rows, :width] = gate_c
            turned_table[part, rows, width:] = (gate_g * vector).astype(jnp.bfloat16)

    own_count = counts[home]
    out[0] = jnp.zeros(out.shape[1:], out.dtype)
    sharpness = 0.5 * ((basis_count - 1) / cutoff) ** 2

    @pl.loop(0, lax.div(own_count + group - 1, group))
    def _(turn):
        first = pl.multiple_of(turn * group, group)
        mine = places[home, pl.ds(first, group), :]

        @pl.loop(0, chunks)
        def _(step):
            columns = pl.ds(pl.multiple_of(step * chunk, chunk), chunk)
            col = step * chunk + lax.broadcasted_iota(jnp.int32, (group, chunk), 1)
            row = first + lax.broadcasted_iota(jnp.int32, (group, chunk), 0)
            unused = jnp.logical_or(col == own_start + row, col >= total)
            offset = [place_rows[k : k + 1, columns] - mine[:, k : k + 1] for k in range(3)]
            square = offset[0] * offset[0] + offset[1] * offset[1] + offset[2] * offset[2]
            distance = jnp.sqrt(square + jnp.where(unused, 1.0, 0.0))
            inverse = 1.0 / distance
            smooth = 0.5 * (jnp.cos(math.pi / cutoff * distance) + 1.0)
            weight = jnp.where(
                jnp.logical_and(distance < cutoff, jnp.logical_not(unused)), smooth, 0.0
            )
            centers = lax.broadcasted_iota(jnp.int32, (1, basis_count, chunk), 1).astype(
                jnp.float32
            ) * (cutoff / (basis_count - 1))
            gap = distance[:, None, :] - centers
            basis = jnp.exp(-sharpness * gap * gap).reshape(group * basis_count, chunk)
            half = jnp.dot(
                radial_block[...], basis.astype(jnp.bfloat16), preferred_element_type=jnp.float32
            ).reshape(group, hidden_width, chunk) + radial_bias[...][None]
            active = (half + half * jnp.tanh(half)) * weight[:, None, :]
            edges[0, :, columns] = active.reshape(group * hidden_width, chunk).astype(jnp.bfloat16)
            for k in range(3):
                unit = (offset[k] * inverse)[:, None, :]
                edges[k + 1, :, columns] = (
                    (active * unit).reshape(group * hidden_width, chunk).astype(jnp.bfloat16)
                )

        for used in range(1, max_chunks + 1):

            @pl.when(chunks == used)
            def _(used=used):
                span = used * chunk

                def contracted(left, right, filters):
                    product = jnp.dot(left, right, preferred_element_type=jnp.float32)
                    product = product.reshape(group, hidden_width, 2 * width)
                    return (
                        jnp.sum(product[:, :, :width] * filters[0], axis=1),
                        jnp.sum(product[:, :, width:] * filters[1], axis=1),
                    )

                bank = [
                    radial_out[:, part * width : (part + 1) * width].astype(jnp.float32)[None]
                    for part in range(4)
                ]
                flat = edges[0, :, :span]
                scalar, vector0 = contracted(flat, plain_table[:span, : 2 * width], (bank[0], bank[1]))
                vector1, vector2 = contracted(flat, plain_table[:span, 2 * width :], (bank[1], bank[1]))
                vectors = [vector0, vector1, vector2]
                for k in range(3):
                    along, project = contracted(
                        edges[k + 1, :, :span], turned_table[k, :span, :], (bank[2], bank[3])
                    )
                    vectors[k] = vectors[k] + along
                    scalar = scalar + project
                receivers = first + lax.broadcasted_iota(jnp.int32, (group, width), 0)
                alive = receivers < own_count
                for part, change in enumerate([scalar] + vectors):
                    before = near_state[part, pl.ds(own_start + first, group), :]
                    after = jnp.where(alive, before + message_scale * change, 0.0)
                    out[0, pl.ds(first, group), part * width : (part + 1) * width] = after


def layer_update(cells_shape, counts, places, feats, params):
    cells_wide, cells_deep, cells_tall = cells_shape
    radial_in, radial_bias, radial_out, atom_in, atom_bias, atom_out = params
    total_cells = cells_wide * cells_deep * cells_tall
    slots = feats.shape[1]
    width = feats.shape[2] // 4
    hidden_width = radial_in.shape[1]
    max_chunks = -(-27 * slots // chunk)
    radial_block = jnp.kron(jnp.eye(group, dtype=jnp.float32), 0.5 * radial_in.astype(jnp.float32).T)
    span = max_chunks * chunk
    store = 27 * slots + chunk + slots
    store = -(-store // 8) * 8
    vmem = pl.BlockSpec(memory_space=pltpu.VMEM)
    return pl.pallas_call(
        functools.partial(layer_kernel, (cells_deep, cells_tall), max_chunks),
        grid=(total_cells,),
        out_shape=jax.ShapeDtypeStruct((total_cells, slots, 4 * width), jnp.float32),
        in_specs=[pl.BlockSpec(memory_space=pltpu.SMEM)] + [vmem] * 8,
        out_specs=pl.BlockSpec((1, slots, 4 * width), lambda i: (i, 0, 0)),
        scratch_shapes=[
            pltpu.VMEM((store, width), jnp.float32),
            pltpu.VMEM((4, store, width), jnp.float32),
            pltpu.VMEM((8, span), jnp.float32),
            pltpu.VMEM((4, group * hidden_width, span), jnp.bfloat16),
            pltpu.VMEM((span, 4 * width), jnp.bfloat16),
            pltpu.VMEM((3, span, 2 * width), jnp.bfloat16),
        ],
        compiler_params=pltpu.CompilerParams(vmem_limit_bytes=56 << 20),
        name="message_layer",
    )(
        counts,
        places,
        feats,
        radial_block.astype(jnp.bfloat16),
        jnp.broadcast_to(0.5 * radial_bias[:, None], (hidden_width, chunk)),
        radial_out,
        (0.5 * atom_in.astype(jnp.float32)).astype(jnp.bfloat16),
        0.5 * atom_bias[None, :],
        atom_out,
    )


def summed(value, axes):
    for axis in axes:
        count = lax.axis_size(axis)
        if count & (count - 1):
            value = lax.psum(value, axis)
            continue
        step = 1
        while step < count:
            value = value + lax.ppermute(value, axis, [(i, i ^ step) for i in range(count)])
            step *= 2
    return value


def on_device(
    positions,
    counts,
    scalars,
    vectors,
    radial_in,
    radial_bias,
    radial_out,
    atom_in,
    atom_bias,
    atom_out,
    readout_in,
    readout_out,
):
    cells_wide, cells_deep, cells_tall, slots, width = scalars.shape
    cells_shape = (cells_wide, cells_deep, cells_tall)
    sides = (("gy", 1), ("gx", 0), ("gz", 2))
    live = (
        lax.broadcasted_iota(jnp.int32, cells_shape + (slots,), 3) < counts[:, :, :, None]
    ).astype(jnp.float32)
    level = jnp.broadcast_to(counts.astype(jnp.float32)[..., None, None], cells_shape + (1, slots))
    geometry = extended(jnp.concatenate([positions, level], axis=3), sides, 1)
    near_counts = geometry[:, :, :, 3, 0].astype(jnp.int32).reshape(-1)
    places = geometry.reshape((-1,) + geometry.shape[3:]).transpose(0, 2, 1)
    places = jnp.pad(places, ((0, 0), (0, 0), (0, width - places.shape[2])))
    state = jnp.concatenate(
        [scalars, vectors.reshape(cells_shape + (slots, 3 * width))], axis=-1
    )
    for layer in range(radial_in.shape[0]):
        params = (
            radial_in[layer],
            radial_bias[layer],
            radial_out[layer],
            atom_in[layer],
            atom_bias[layer],
            atom_out[layer],
        )
        feats = extended(state, sides, 1)
        state = layer_update(
            cells_shape, near_counts, places, feats.reshape(-1, slots, 4 * width), params
        )
        state = state.astype(jnp.bfloat16).reshape(cells_shape + (slots, 4 * width))
    scalar_state = state[..., :width]
    vector_state = state[..., width:].reshape(cells_shape + (slots, 3, width))
    readout_hidden = jax.nn.silu(
        jnp.dot(scalar_state.reshape(-1, width), readout_in, preferred_element_type=jnp.float32)
    )
    atom_energy = jnp.sum(readout_hidden * readout_out, axis=-1) * live.reshape(-1)
    energy = summed(jnp.sum(atom_energy).reshape(1), ("gx", "gy", "gz"))
    return (scalar_state, vector_state, energy)


def solution(mesh):
    block = P("gx", "gy", "gz")
    in_specs = (block,) * 4 + (P(),) * 8
    out_specs = (block, block, P())
    return jax.shard_map(
        on_device, mesh=mesh, in_specs=in_specs, out_specs=out_specs, check_vma=False
    )
```

time: 419 us -> 121 us (0.29)
  local copies, waits for them, and re-layouts: 149 us -> 12.9 us
  matrix products: 67.1 us -> 0.17 us
  other arithmetic: 58.9 us -> 7.29 us
  blocking collectives: 41.1 us -> 0 us
  loops' own time: 34.5 us -> 0 us
  starting transfers between devices: 16.8 us -> 46.1 us
  waiting for transfers between devices: 49.4 us -> 28.5 us
  Pallas kernels: 0 us -> 19.3 us
  between operations: 0.87 us -> 5.87 us
    dot_general x130 -> x0, matrix products: 66.2 us -> none  [the longest x32 17.8 us: receiver_block(): lax.dot_general(edge_turned, pair_g, (((1, 2), (0, 1)), ((), ())), prefer...]
    dynamic_slice x108 -> x0, local copies, waits for them, and re-layouts: 41.3 us -> none  [the longest x32 21 us: cell_deltas(): lax.map(one_block, jnp.arange(8, dtype=jnp.int32))]
    psum x1 -> x0, blocking collectives: 41.1 us -> none  [on_device(): energy = lax.psum(local_energy, ('gx', 'gy', 'gz')).reshape(1)]
    reshape x66 -> x2, local copies, waits for them, and re-layouts: 40.3 us -> 0.07 us  [the longest x1 0.05 us: on_device(): vectors.reshape(cells_shape + (slots, 3 * width))]
    another operation x6 -> x0, loops' own time: 34.5 us -> none  [the longest x4 26.3 us: cell_deltas(): lax.map(one_block, jnp.arange(8, dtype=jnp.int32))]
    while x400 -> x0, local copies, waits for them, and re-layouts: 32.5 us -> none
    ppermute x9, waiting for transfers between devices: 33.3 us -> 7.72 us  [extended(): lax.ppermute(lax.slice_in_dim(block, 0, width, axis=dim), axis, backward)]
    dynamic_update_slice x64 -> x0, other arithmetic: 19.8 us -> none  [cell_deltas(): lax.map(one_block, jnp.arange(8, dtype=jnp.int32))]
  transfers between devices with their start and end apart: 18 -> 23, of which waited for: 13 -> 14; matrix products, arithmetic and copies ran while one was open for 2% -> 10% of each run, Pallas kernels for 0% -> 0%
where the time goes in v1:
time: 121 us; the launch traced here: 120 us
  starting transfers between devices  46.1 us (38%)
  waiting for transfers between devices  28.5 us (24%)
  Pallas kernels  19.3 us (16%)
  local copies, waits for them, and re-layouts  12.9 us (11%)
  other arithmetic  7.29 us (6%)
  between operations  5.87 us (5%)
    pallas_call x2, Pallas kernels, layer_update(): pl.pallas_call(functools.partial(layer_kernel, (cells_deep, cells_tall),...  19.3 us
    ppermute x5, starting transfers between devices, summed(): lax.ppermute(value, axis, [(i, i ^ step) for i in range(count)])  17.6 us
    ppermute x9, starting transfers between devices, extended(): lax.ppermute(lax.slice_in_dim(block, 0, width, axis=dim), axis, backward)  15.7 us
    ppermute x9, waiting for transfers between devices, extended(): lax.ppermute(lax.slice_in_dim(block, block.shape[dim] - width, None, axis...  14.5 us
    ppermute x9, starting transfers between devices, extended(): lax.ppermute(lax.slice_in_dim(block, block.shape[dim] - width, None, axis...  12.7 us
    ppermute x9, waiting for transfers between devices, extended(): lax.ppermute(lax.slice_in_dim(block, 0, width, axis=dim), axis, backward)  7.72 us
    ppermute x5, waiting for transfers between devices, summed(): lax.ppermute(value, axis, [(i, i ^ step) for i in range(count)])  6.32 us
    concatenate x3, local copies, waits for them, and re-layouts, extended(): block = jnp.concatenate([low, block, high], axis=dim)  2.51 us
  transfers between devices with their start and end apart: 23, of which 14 were waited for; matrix products, arithmetic and copies ran while one was open for 10% of the time, Pallas kernels for 0%

profile of v1, /device:TPU:0, one launch (start us, length us, event | category | flops | bytes accessed | tf_op | source)
XLA Modules:
  0.0 120.2 jit_solution(8037249228440948348)
XLA Ops:
  2.3 3.1 %collective-permute-start.6 = (bf16[2,1,1,32,512]{4,3,0,2,1:T(8,128)(2,1)S(1)}, bf16[2,1,1,32,512]{4,3,0,2,1:T(8,128)(2,1)S(1)}, u32[]{:S(2)}, u32[]{:S(2)}) collective-permute-start(bf16[2,1,1,32,512]{4,3,0,2,1:T(8,128)(2,1)S(1)} %pad_maximum_fusion.7), channel_id=1, source_target_pairs={{0,4},{4,8},{8,12},{12,0},{1,5},{5,9},{9,13},{13,1},{2,6},{6,10},{... | collective-permute-start | bytes 196616 | tf_op jit(solution)/shard_map/ppermute | solution.py:23
  5.4 2.1 %collective-permute-start.7 = (bf16[2,1,1,32,512]{4,3,0,2,1:T(8,128)(2,1)S(1)}, bf16[2,1,1,32,512]{4,3,0,2,1:T(8,128)(2,1)S(1)}, u32[]{:S(2)}, u32[]{:S(2)}) collective-permute-start(bf16[2,1,1,32,512]{4,3,0,2,1:T(8,128)(2,1)S(1)} %pad_maximum_fusion.7), channel_id=1, source_target_pairs={{4,0},{8,4},{12,8},{0,12},{5,1},{9,5},{13,9},{1,13},{6,2},{10,6},{... | collective-permute-start | bytes 196616 | tf_op jit(solution)/shard_map/ppermute | solution.py:26
  8.9 3.8 %collective-permute-start.1 = (f32[2,1,1,4,32]{4,2,3,1,0:T(1,128)S(1)}, f32[2,1,1,4,32]{4,2,3,1,0:T(1,128)S(1)}, u32[]{:S(2)}, u32[]{:S(2)}) collective-permute-start(f32[2,1,1,4,32]{4,2,3,1,0:T(1,128)S(1)} %pad_maximum_fusion.10), channel_id=1, source_target_pairs={{4,0},{8,4},{12,8},{0,12},{5,1},{9,5},{13,9},{1,13},{6,2},{10,6},{... | collective-permute-start | bytes 3080 | tf_op jit(solution)/shard_map/ppermute | solution.py:26
  13.4 1.7 %slice_bitcast_fusion = (bf16[128,512]{1,0:T(8,128)(2,1)}, bf16[128,512]{1,0:T(8,128)(2,1)}) fusion(bf16[2,128,512]{2,1,0:T(8,128)(2,1)} %param.21), kind=kLoop, calls=%fused_computation.8 | loop fusion | bytes 524288 | tf_op jit(solution)/shard_map/squeeze | solution.py:281
  17.5 1.7 %collective-permute-start.2 = (f32[1,3,1,4,32]{4,2,3,1,0:T(1,128)S(1)}, f32[1,3,1,4,32]{4,2,3,1,0:T(1,128)S(1)}, u32[]{:S(2)}, u32[]{:S(2)}) collective-permute-start(f32[1,3,1,4,32]{4,2,3,1,0:T(1,128)S(1)} %get-tuple-element.21), channel_id=1, source_target_pairs={{0,16},{16,0},{1,17},{17,1},{2,18},{18,2},{3,19},{19,3},{4,20},{20... | collective-permute-start | bytes 4616 | tf_op jit(solution)/shard_map/ppermute | solution.py:23
  19.6 1.7 %collective-permute-start.8 = (bf16[1,3,1,32,512]{4,3,0,2,1:T(8,128)(2,1)S(1)}, bf16[1,3,1,32,512]{4,3,0,2,1:T(8,128)(2,1)S(1)}, u32[]{:S(2)}, u32[]{:S(2)}) collective-permute-start(bf16[1,3,1,32,512]{4,3,0,2,1:T(8,128)(2,1)S(1)} %get-tuple-element.13), channel_id=1, source_target_pairs={{0,16},{16,0},{1,17},{17,1},{2,18},{18,2},{3,19},{19,3},{4,20},{20... | collective-permute-start | bytes 294920 | tf_op jit(solution)/shard_map/ppermute | solution.py:23
  23.0 1.7 %collective-permute-start.5 = (f32[4,3,1,4,32]{4,2,3,1,0:T(1,128)S(1)}, f32[4,3,1,4,32]{4,2,3,1,0:T(1,128)S(1)}, u32[]{:S(2)}, u32[]{:S(2)}) collective-permute-start(f32[4,3,1,4,32]{4,2,3,1,0:T(1,128)S(1)} %pad_maximum_fusion.8), channel_id=1, source_target_pairs={{1,0},{2,1},{3,2},{0,3},{5,4},{6,5},{7,6},{4,7},{9,8},{10,9},{11,1... | collective-permute-start | bytes 18440 | tf_op jit(solution)/shard_map/ppermute | solution.py:26
  26.1 1.7 %collective-permute-start.11 = (bf16[4,3,1,32,512]{4,3,0,2,1:T(8,128)(2,1)S(1)}, bf16[4,3,1,32,512]{4,3,0,2,1:T(8,128)(2,1)S(1)}, u32[]{:S(2)}, u32[]{:S(2)}) collective-permute-start(bf16[4,3,1,32,512]{4,3,0,2,1:T(8,128)(2,1)S(1)} %pad_maximum_fusion.2), channel_id=1, source_target_pairs={{1,0},{2,1},{3,2},{0,3},{5,4},{6,5},{7,6},{4,7},{9,8},{10,9},{11,1... | collective-permute-start | bytes 1179656 | tf_op jit(solution)/shard_map/ppermute | solution.py:26
  31.4 4.3 %collective-permute-done.10 = bf16[4,3,1,32,512]{4,3,0,2,1:T(8,128)(2,1)S(1)} collective-permute-done((bf16[4,3,1,32,512]{4,3,0,2,1:T(8,128)(2,1)S(1)}, bf16[4,3,1,32,512]{4,3,0,2,1:T(8,128)(2,1)S(1)}, u32[]{:S(2)}, u32[]{:S(2)}) %collective-permute-start.10) | collective-permute-done | bytes 393248 | tf_op jit(solution)/shard_map/ppermute | solution.py:23
  38.4 9.7 %message_layer.2 = f32[2,32,512]{2,1,0:T(8,128)} custom-call(s32[36]{0:T(128)} %convert_element_type.71.counts, f32[36,32,128]{2,1,0:T(8,128)} %pad.4.places, bf16[36,32,512]{2,1,0:T(8,128)(2,1)} %bitcast.62, bf16[512,64]{1,0:T(8,128)(2,1)} %copy.25.radial_block, f32[64,256]{1,0:T(8,128)} %broadcast_in_dim.28.radial_bias, ...), custom_call_target="tpu_custom_call" | custom-call | tf_op jit(solution)/shard_map/message_layer/pallas_call | solution.py:204
  49.1 3.8 %collective-permute-start.13 = (bf16[2,1,1,32,512]{4,3,0,2,1:T(8,128)(2,1)S(1)}, bf16[2,1,1,32,512]{4,3,0,2,1:T(8,128)(2,1)S(1)}, u32[]{:S(2)}, u32[]{:S(2)}) collective-permute-start(bf16[2,1,1,32,512]{4,3,0,2,1:T(8,128)(2,1)S(1)} %convert_bitcast_fusion.1), channel_id=1, source_target_pairs={{4,0},{8,4},{12,8},{0,12},{5,1},{9,5},{13,9},{1,13},{6,2},{10,6},{... | collective-permute-start | bytes 196616 | tf_op jit(solution)/shard_map/ppermute | solution.py:26
  52.9 2.9 %collective-permute-done.12 = bf16[2,1,1,32,512]{4,3,0,2,1:T(8,128)(2,1)S(1)} collective-permute-done((bf16[2,1,1,32,512]{4,3,0,2,1:T(8,128)(2,1)S(1)}, bf16[2,1,1,32,512]{4,3,0,2,1:T(8,128)(2,1)S(1)}, u32[]{:S(2)}, u32[]{:S(2)}) %collective-permute-start.12) | collective-permute-done | bytes 65568 | tf_op jit(solution)/shard_map/ppermute | solution.py:23
  55.9 6.0 %collective-permute-start.14 = (bf16[1,3,1,32,512]{4,3,0,2,1:T(8,128)(2,1)S(1)}, bf16[1,3,1,32,512]{4,3,0,2,1:T(8,128)(2,1)S(1)}, u32[]{:S(2)}, u32[]{:S(2)}) collective-permute-start(bf16[1,3,1,32,512]{4,3,0,2,1:T(8,128)(2,1)S(1)} %get-tuple-element.11), channel_id=1, source_target_pairs={{0,16},{16,0},{1,17},{17,1},{2,18},{18,2},{3,19},{19,3},{4,20},{20... | collective-permute-start | bytes 294920 | tf_op jit(solution)/shard_map/ppermute | solution.py:23
  61.9 2.5 %collective-permute-done.14 = bf16[1,3,1,32,512]{4,3,0,2,1:T(8,128)(2,1)S(1)} collective-permute-done((bf16[1,3,1,32,512]{4,3,0,2,1:T(8,128)(2,1)S(1)}, bf16[1,3,1,32,512]{4,3,0,2,1:T(8,128)(2,1)S(1)}, u32[]{:S(2)}, u32[]{:S(2)}) %collective-permute-start.14) | collective-permute-done | bytes 98336 | tf_op jit(solution)/shard_map/ppermute | solution.py:23
  64.4 2.0 %collective-permute-done.15 = bf16[1,3,1,32,512]{4,3,0,2,1:T(8,128)(2,1)S(1)} collective-permute-done((bf16[1,3,1,32,512]{4,3,0,2,1:T(8,128)(2,1)S(1)}, bf16[1,3,1,32,512]{4,3,0,2,1:T(8,128)(2,1)S(1)}, u32[]{:S(2)}, u32[]{:S(2)}) %collective-permute-start.15) | collective-permute-done | bytes 98336 | tf_op jit(solution)/shard_map/ppermute | solution.py:26
  66.6 1.7 %collective-permute-start.17 = (bf16[4,3,1,32,512]{4,3,0,2,1:T(8,128)(2,1)S(1)}, bf16[4,3,1,32,512]{4,3,0,2,1:T(8,128)(2,1)S(1)}, u32[]{:S(2)}, u32[]{:S(2)}) collective-permute-start(bf16[4,3,1,32,512]{4,3,0,2,1:T(8,128)(2,1)S(1)} %pad_maximum_fusion.3), channel_id=1, source_target_pairs={{1,0},{2,1},{3,2},{0,3},{5,4},{6,5},{7,6},{4,7},{9,8},{10,9},{11,1... | collective-permute-start | bytes 1179656 | tf_op jit(solution)/shard_map/ppermute | solution.py:26
  69.5 4.7 %collective-permute-done.16 = bf16[4,3,1,32,512]{4,3,0,2,1:T(8,128)(2,1)S(1)} collective-permute-done((bf16[4,3,1,32,512]{4,3,0,2,1:T(8,128)(2,1)S(1)}, bf16[4,3,1,32,512]{4,3,0,2,1:T(8,128)(2,1)S(1)}, u32[]{:S(2)}, u32[]{:S(2)}) %collective-permute-start.16) | collective-permute-done | bytes 393248 | tf_op jit(solution)/shard_map/ppermute | solution.py:23
  74.2 2.5 %collective-permute-done.17 = bf16[4,3,1,32,512]{4,3,0,2,1:T(8,128)(2,1)S(1)} collective-permute-done((bf16[4,3,1,32,512]{4,3,0,2,1:T(8,128)(2,1)S(1)}, bf16[4,3,1,32,512]{4,3,0,2,1:T(8,128)(2,1)S(1)}, u32[]{:S(2)}, u32[]{:S(2)}) %collective-permute-start.17) | collective-permute-done | bytes 393248 | tf_op jit(solution)/shard_map/ppermute | solution.py:26
  78.6 9.7 %message_layer.3 = f32[2,32,512]{2,1,0:T(8,128)} custom-call(s32[36]{0:T(128)} %convert_element_type.71.counts, f32[36,32,128]{2,1,0:T(8,128)} %pad.4.places, bf16[36,32,512]{2,1,0:T(8,128)(2,1)} %bitcast.61, bf16[512,64]{1,0:T(8,128)(2,1)} %copy.27.radial_block, f32[64,256]{1,0:T(8,128)} %broadcast_in_dim.29.radial_bias, ...), custom_call_target="tpu_custom_call" | custom-call | tf_op jit(solution)/shard_map/message_layer/pallas_call | solution.py:204
  90.6 6.6 %collective-permute-start.18 = (f32[1]{0:T(128)}, f32[1]{0:T(128)}, u32[]{:S(2)}, u32[]{:S(2)}) collective-permute-start(f32[1]{0:T(128)} %bitcast.23), channel_id=1, source_target_pairs={{0,16},{16,0},{1,17},{17,1},{2,18},{18,2},{3,19},{19,3},{4,20},{20... | collective-permute-start | bytes 20 | tf_op jit(solution)/shard_map/ppermute | solution.py:241
  101.5 2.2 %collective-permute-done.19 = f32[1]{0:T(128)} collective-permute-done((f32[1]{0:T(128)}, f32[1]{0:T(128)}, u32[]{:S(2)}, u32[]{:S(2)}) %collective-permute-start.19) | collective-permute-done | bytes 36 | tf_op jit(solution)/shard_map/ppermute | solution.py:241
  104.3 1.9 %collective-permute-start.20 = (f32[1]{0:T(128)}, f32[1]{0:T(128)}, u32[]{:S(2)}, u32[]{:S(2)}) collective-permute-start(f32[1]{0:T(128)} %add.23), channel_id=1, source_target_pairs={{0,8},{4,12},{8,0},{12,4},{1,9},{5,13},{9,1},{13,5},{2,10},{6,14},... | collective-permute-start | bytes 20 | tf_op jit(solution)/shard_map/ppermute | solution.py:241
  106.2 2.6 %collective-permute-done.20 = f32[1]{0:T(128)} collective-permute-done((f32[1]{0:T(128)}, f32[1]{0:T(128)}, u32[]{:S(2)}, u32[]{:S(2)}) %collective-permute-start.20) | collective-permute-done | bytes 36 | tf_op jit(solution)/shard_map/ppermute | solution.py:241
  111.3 6.9 %collective-permute-start.22 = (f32[1]{0:T(128)}, f32[1]{0:T(128)}, u32[]{:S(2)}, u32[]{:S(2)}) collective-permute-start(f32[1]{0:T(128)} %add.25), channel_id=1, source_target_pairs={{0,2},{1,3},{2,0},{3,1},{4,6},{5,7},{6,4},{7,5},{8,10},{9,11},{10,... | collective-permute-start | bytes 20 | tf_op jit(solution)/shard_map/ppermute | solution.py:241
  (90 shorter events, 26.7 us)
Async XLA Ops:
  0.6 89.2 %copy-start = (bf16[128,64]{0,1:T(8,128)(2,1)S(1)}, bf16[128,64]{0,1:T(8,128)(2,1)}, u32[]{:S(2)}) copy-start(bf16[128,64]{0,1:T(8,128)(2,1)} %param.22) | copy-start | bytes 49156
  2.3 17.2 %collective-permute-start.6 = (bf16[2,1,1,32,512]{4,3,0,2,1:T(8,128)(2,1)S(1)}, bf16[2,1,1,32,512]{4,3,0,2,1:T(8,128)(2,1)S(1)}, u32[]{:S(2)}, u32[]{:S(2)}) collective-permute-start(bf16[2,1,1,32,512]{4,3,0,2,1:T(8,128)(2,1)S(1)} %pad_maximum_fusion.7), channel_id=1, source_target_pairs={{0,4},{4,8},{8,12},{12,0},{1,5},{5,9},{9,13},{13,1},{2,6},{6,10},{... | collective-permute-start | bytes 196616 | tf_op jit(solution)/shard_map/ppermute | solution.py:23
  5.4 14.2 %collective-permute-start.7 = (bf16[2,1,1,32,512]{4,3,0,2,1:T(8,128)(2,1)S(1)}, bf16[2,1,1,32,512]{4,3,0,2,1:T(8,128)(2,1)S(1)}, u32[]{:S(2)}, u32[]{:S(2)}) collective-permute-start(bf16[2,1,1,32,512]{4,3,0,2,1:T(8,128)(2,1)S(1)} %pad_maximum_fusion.7), channel_id=1, source_target_pairs={{4,0},{8,4},{12,8},{0,12},{5,1},{9,5},{13,9},{1,13},{6,2},{10,6},{... | collective-permute-start | bytes 196616 | tf_op jit(solution)/shard_map/ppermute | solution.py:26
  8.9 8.5 %collective-permute-start = (f32[2,1,1,4,32]{4,2,3,1,0:T(1,128)S(1)}, f32[2,1,1,4,32]{4,2,3,1,0:T(1,128)S(1)}, u32[]{:S(2)}, u32[]{:S(2)}) collective-permute-start(f32[2,1,1,4,32]{4,2,3,1,0:T(1,128)S(1)} %pad_maximum_fusion.10), channel_id=1, source_target_pairs={{0,4},{4,8},{8,12},{12,0},{1,5},{5,9},{9,13},{13,1},{2,6},{6,10},{... | collective-permute-start | bytes 3080 | tf_op jit(solution)/shard_map/ppermute | solution.py:23
  8.9 8.5 %collective-permute-start.1 = (f32[2,1,1,4,32]{4,2,3,1,0:T(1,128)S(1)}, f32[2,1,1,4,32]{4,2,3,1,0:T(1,128)S(1)}, u32[]{:S(2)}, u32[]{:S(2)}) collective-permute-start(f32[2,1,1,4,32]{4,2,3,1,0:T(1,128)S(1)} %pad_maximum_fusion.10), channel_id=1, source_target_pairs={{4,0},{8,4},{12,8},{0,12},{5,1},{9,5},{13,9},{1,13},{6,2},{10,6},{... | collective-permute-start | bytes 3080 | tf_op jit(solution)/shard_map/ppermute | solution.py:26
  17.5 4.2 %collective-permute-start.2 = (f32[1,3,1,4,32]{4,2,3,1,0:T(1,128)S(1)}, f32[1,3,1,4,32]{4,2,3,1,0:T(1,128)S(1)}, u32[]{:S(2)}, u32[]{:S(2)}) collective-permute-start(f32[1,3,1,4,32]{4,2,3,1,0:T(1,128)S(1)} %get-tuple-element.21), channel_id=1, source_target_pairs={{0,16},{16,0},{1,17},{17,1},{2,18},{18,2},{3,19},{19,3},{4,20},{20... | collective-permute-start | bytes 4616 | tf_op jit(solution)/shard_map/ppermute | solution.py:23
  19.2 3.7 %collective-permute-start.3 = (f32[1,3,1,4,32]{4,2,3,1,0:T(1,128)S(1)}, f32[1,3,1,4,32]{4,2,3,1,0:T(1,128)S(1)}, u32[]{:S(2)}, u32[]{:S(2)}) collective-permute-start(f32[1,3,1,4,32]{4,2,3,1,0:T(1,128)S(1)} %get-tuple-element.22), channel_id=1, source_target_pairs={{16,0},{0,16},{17,1},{1,17},{18,2},{2,18},{19,3},{3,19},{20,4},{4,... | collective-permute-start | bytes 4616 | tf_op jit(solution)/shard_map/ppermute | solution.py:26
  19.6 5.1 %collective-permute-start.8 = (bf16[1,3,1,32,512]{4,3,0,2,1:T(8,128)(2,1)S(1)}, bf16[1,3,1,32,512]{4,3,0,2,1:T(8,128)(2,1)S(1)}, u32[]{:S(2)}, u32[]{:S(2)}) collective-permute-start(bf16[1,3,1,32,512]{4,3,0,2,1:T(8,128)(2,1)S(1)} %get-tuple-element.13), channel_id=1, source_target_pairs={{0,16},{16,0},{1,17},{17,1},{2,18},{18,2},{3,19},{19,3},{4,20},{20... | collective-permute-start | bytes 294920 | tf_op jit(solution)/shard_map/ppermute | solution.py:23
  21.4 4.6 %collective-permute-start.9 = (bf16[1,3,1,32,512]{4,3,0,2,1:T(8,128)(2,1)S(1)}, bf16[1,3,1,32,512]{4,3,0,2,1:T(8,128)(2,1)S(1)}, u32[]{:S(2)}, u32[]{:S(2)}) collective-permute-start(bf16[1,3,1,32,512]{4,3,0,2,1:T(8,128)(2,1)S(1)} %get-tuple-element.14), channel_id=1, source_target_pairs={{16,0},{0,16},{17,1},{1,17},{18,2},{2,18},{19,3},{3,19},{20,4},{4,... | collective-permute-start | bytes 294920 | tf_op jit(solution)/shard_map/ppermute | solution.py:26
  23.0 6.3 %collective-permute-start.4 = (f32[4,3,1,4,32]{4,2,3,1,0:T(1,128)S(1)}, f32[4,3,1,4,32]{4,2,3,1,0:T(1,128)S(1)}, u32[]{:S(2)}, u32[]{:S(2)}) collective-permute-start(f32[4,3,1,4,32]{4,2,3,1,0:T(1,128)S(1)} %pad_maximum_fusion.8), channel_id=1, source_target_pairs={{0,1},{1,2},{2,3},{3,0},{4,5},{5,6},{6,7},{7,4},{8,9},{9,10},{10,1... | collective-permute-start | bytes 18440 | tf_op jit(solution)/shard_map/ppermute | solution.py:23
  23.0 6.2 %collective-permute-start.5 = (f32[4,3,1,4,32]{4,2,3,1,0:T(1,128)S(1)}, f32[4,3,1,4,32]{4,2,3,1,0:T(1,128)S(1)}, u32[]{:S(2)}, u32[]{:S(2)}) collective-permute-start(f32[4,3,1,4,32]{4,2,3,1,0:T(1,128)S(1)} %pad_maximum_fusion.8), channel_id=1, source_target_pairs={{1,0},{2,1},{3,2},{0,3},{5,4},{6,5},{7,6},{4,7},{9,8},{10,9},{11,1... | collective-permute-start | bytes 18440 | tf_op jit(solution)/shard_map/ppermute | solution.py:26
  26.0 9.7 %collective-permute-start.10 = (bf16[4,3,1,32,512]{4,3,0,2,1:T(8,128)(2,1)S(1)}, bf16[4,3,1,32,512]{4,3,0,2,1:T(8,128)(2,1)S(1)}, u32[]{:S(2)}, u32[]{:S(2)}) collective-permute-start(bf16[4,3,1,32,512]{4,3,0,2,1:T(8,128)(2,1)S(1)} %pad_maximum_fusion.2), channel_id=1, source_target_pairs={{0,1},{1,2},{2,3},{3,0},{4,5},{5,6},{6,7},{7,4},{8,9},{9,10},{10,1... | collective-permute-start | bytes 1179656 | tf_op jit(solution)/shard_map/ppermute | solution.py:23
  26.1 10.4 %collective-permute-start.11 = (bf16[4,3,1,32,512]{4,3,0,2,1:T(8,128)(2,1)S(1)}, bf16[4,3,1,32,512]{4,3,0,2,1:T(8,128)(2,1)S(1)}, u32[]{:S(2)}, u32[]{:S(2)}) collective-permute-start(bf16[4,3,1,32,512]{4,3,0,2,1:T(8,128)(2,1)S(1)} %pad_maximum_fusion.2), channel_id=1, source_target_pairs={{1,0},{2,1},{3,2},{0,3},{5,4},{6,5},{7,6},{4,7},{9,8},{10,9},{11,1... | collective-permute-start | bytes 1179656 | tf_op jit(solution)/shard_map/ppermute | solution.py:26
  49.0 6.8 %collective-permute-start.12 = (bf16[2,1,1,32,512]{4,3,0,2,1:T(8,128)(2,1)S(1)}, bf16[2,1,1,32,512]{4,3,0,2,1:T(8,128)(2,1)S(1)}, u32[]{:S(2)}, u32[]{:S(2)}) collective-permute-start(bf16[2,1,1,32,512]{4,3,0,2,1:T(8,128)(2,1)S(1)} %convert_bitcast_fusion.1), channel_id=1, source_target_pairs={{0,4},{4,8},{8,12},{12,0},{1,5},{5,9},{9,13},{13,1},{2,6},{6,10},{... | collective-permute-start | bytes 196616 | tf_op jit(solution)/shard_map/ppermute | solution.py:23
  49.1 6.8 %collective-permute-start.13 = (bf16[2,1,1,32,512]{4,3,0,2,1:T(8,128)(2,1)S(1)}, bf16[2,1,1,32,512]{4,3,0,2,1:T(8,128)(2,1)S(1)}, u32[]{:S(2)}, u32[]{:S(2)}) collective-permute-start(bf16[2,1,1,32,512]{4,3,0,2,1:T(8,128)(2,1)S(1)} %convert_bitcast_fusion.1), channel_id=1, source_target_pairs={{4,0},{8,4},{12,8},{0,12},{5,1},{9,5},{13,9},{1,13},{6,2},{10,6},{... | collective-permute-start | bytes 196616 | tf_op jit(solution)/shard_map/ppermute | solution.py:26
  55.9 8.6 %collective-permute-start.14 = (bf16[1,3,1,32,512]{4,3,0,2,1:T(8,128)(2,1)S(1)}, bf16[1,3,1,32,512]{4,3,0,2,1:T(8,128)(2,1)S(1)}, u32[]{:S(2)}, u32[]{:S(2)}) collective-permute-start(bf16[1,3,1,32,512]{4,3,0,2,1:T(8,128)(2,1)S(1)} %get-tuple-element.11), channel_id=1, source_target_pairs={{0,16},{16,0},{1,17},{17,1},{2,18},{18,2},{3,19},{19,3},{4,20},{20... | collective-permute-start | bytes 294920 | tf_op jit(solution)/shard_map/ppermute | solution.py:23
  61.8 4.6 %collective-permute-start.15 = (bf16[1,3,1,32,512]{4,3,0,2,1:T(8,128)(2,1)S(1)}, bf16[1,3,1,32,512]{4,3,0,2,1:T(8,128)(2,1)S(1)}, u32[]{:S(2)}, u32[]{:S(2)}) collective-permute-start(bf16[1,3,1,32,512]{4,3,0,2,1:T(8,128)(2,1)S(1)} %get-tuple-element.12), channel_id=1, source_target_pairs={{16,0},{0,16},{17,1},{1,17},{18,2},{2,18},{19,3},{3,19},{20,4},{4,... | collective-permute-start | bytes 294920 | tf_op jit(solution)/shard_map/ppermute | solution.py:26
  66.5 7.7 %collective-permute-start.16 = (bf16[4,3,1,32,512]{4,3,0,2,1:T(8,128)(2,1)S(1)}, bf16[4,3,1,32,512]{4,3,0,2,1:T(8,128)(2,1)S(1)}, u32[]{:S(2)}, u32[]{:S(2)}) collective-permute-start(bf16[4,3,1,32,512]{4,3,0,2,1:T(8,128)(2,1)S(1)} %pad_maximum_fusion.3), channel_id=1, source_target_pairs={{0,1},{1,2},{2,3},{3,0},{4,5},{5,6},{6,7},{7,4},{8,9},{9,10},{10,1... | collective-permute-start | bytes 1179656 | tf_op jit(solution)/shard_map/ppermute | solution.py:23
  66.6 10.1 %collective-permute-start.17 = (bf16[4,3,1,32,512]{4,3,0,2,1:T(8,128)(2,1)S(1)}, bf16[4,3,1,32,512]{4,3,0,2,1:T(8,128)(2,1)S(1)}, u32[]{:S(2)}, u32[]{:S(2)}) collective-permute-start(bf16[4,3,1,32,512]{4,3,0,2,1:T(8,128)(2,1)S(1)} %pad_maximum_fusion.3), channel_id=1, source_target_pairs={{1,0},{2,1},{3,2},{0,3},{5,4},{6,5},{7,6},{4,7},{9,8},{10,9},{11,1... | collective-permute-start | bytes 1179656 | tf_op jit(solution)/shard_map/ppermute | solution.py:26
  90.6 8.2 %collective-permute-start.18 = (f32[1]{0:T(128)}, f32[1]{0:T(128)}, u32[]{:S(2)}, u32[]{:S(2)}) collective-permute-start(f32[1]{0:T(128)} %bitcast.23), channel_id=1, source_target_pairs={{0,16},{16,0},{1,17},{17,1},{2,18},{18,2},{3,19},{19,3},{4,20},{20... | collective-permute-start | bytes 20 | tf_op jit(solution)/shard_map/ppermute | solution.py:241
  100.1 3.6 %collective-permute-start.19 = (f32[1]{0:T(128)}, f32[1]{0:T(128)}, u32[]{:S(2)}, u32[]{:S(2)}) collective-permute-start(f32[1]{0:T(128)} %add.22), channel_id=1, source_target_pairs={{0,4},{4,0},{8,12},{12,8},{1,5},{5,1},{9,13},{13,9},{2,6},{6,2},{1... | collective-permute-start | bytes 20 | tf_op jit(solution)/shard_map/ppermute | solution.py:241
  104.3 4.5 %collective-permute-start.20 = (f32[1]{0:T(128)}, f32[1]{0:T(128)}, u32[]{:S(2)}, u32[]{:S(2)}) collective-permute-start(f32[1]{0:T(128)} %add.23), channel_id=1, source_target_pairs={{0,8},{4,12},{8,0},{12,4},{1,9},{5,13},{9,1},{13,5},{2,10},{6,14},... | collective-permute-start | bytes 20 | tf_op jit(solution)/shard_map/ppermute | solution.py:241
  109.5 1.2 %collective-permute-start.21 = (f32[1]{0:T(128)}, f32[1]{0:T(128)}, u32[]{:S(2)}, u32[]{:S(2)}) collective-permute-start(f32[1]{0:T(128)} %add.24), channel_id=1, source_target_pairs={{0,1},{1,0},{2,3},{3,2},{4,5},{5,4},{6,7},{7,6},{8,9},{9,8},{10,11... | collective-permute-start | bytes 20 | tf_op jit(solution)/shard_map/ppermute | solution.py:241
  111.3 7.1 %collective-permute-start.22 = (f32[1]{0:T(128)}, f32[1]{0:T(128)}, u32[]{:S(2)}, u32[]{:S(2)}) collective-permute-start(f32[1]{0:T(128)} %add.25), channel_id=1, source_target_pairs={{0,2},{1,3},{2,0},{3,1},{4,6},{5,7},{6,4},{7,5},{8,10},{9,11},{10,... | collective-permute-start | bytes 20 | tf_op jit(solution)/shard_map/ppermute | solution.py:241
  (7 other events, 113.6 us)

commit v2 on v1

--- a/solution.py
+++ b/solution.py
@@ -14,33 +14,186 @@
 chunk = 256
 
 
-def extended(block, sides, width):
-    for axis, dim in sides:
-        count = lax.axis_size(axis)
-        forward = [(i, i + 1) for i in range(count - 1)]
-        forward.append((count - 1, 0))
-        backward = [(target, source) for source, target in forward]
-        low = lax.ppermute(
-            lax.slice_in_dim(block, block.shape[dim] - width, None, axis=dim), axis, forward
-        )
-        high = lax.ppermute(lax.slice_in_dim(block, 0, width, axis=dim), axis, backward)
-        block = jnp.concatenate([low, block, high], axis=dim)
-    return block
+MESH = pl.DeviceIdType.MESH
+pieces = 4
+sides = (("gy", 1), ("gx", 0), ("gz", 2))
+
+
+def ring(axis):
+    me = lax.axis_index(axis)
+    count = lax.axis_size(axis)
+    return lax.rem(me + 1, count), lax.rem(me + count - 1, count)
+
+
+def halo_kernel(array_count, *refs):
+    blocks = refs[:array_count]
+    pads = refs[array_count : 2 * array_count]
+    local_sem, send_sem, recv_sem = refs[2 * array_count :]
+    dims = blocks[0].shape[:3]
+    around = {axis: ring(axis) for axis, _ in sides}
+    barrier = pltpu.get_barrier_semaphore()
+    for axis, _ in sides:
+        for side in around[axis]:
+            pl.semaphore_signal(barrier, inc=1, device_id={axis: side}, device_id_type=MESH)
+    units = []
+    for block, pad in zip(blocks, pads):
+        lanes = block.shape[-1]
+        cuts = pieces if lanes % (128 * pieces) == 0 else 1
+        for cut in range(cuts):
+            units.append((block, pad, pl.ds(cut * (lanes // cuts), lanes // cuts)))
+    units = units[::-1] if array_count > 1 else units
+    center = tuple(pl.ds(1, extent) for extent in dims)
+    own = []
+    for place, (block, pad) in enumerate(zip(blocks, pads)):
+        own.append(pltpu.make_async_copy(block, pad.at[center], local_sem.at[place]))
+        own[-1].start()
+    pl.semaphore_wait(barrier, 2 * len(sides))
+    sent = {}
+
+    def send(stage, number):
+        block, pad, lanes = units[number]
+        axis, dim = sides[stage]
+        done = [d for _, d in sides[:stage]]
+        extent = dims[dim]
+        for way, (source, target) in enumerate(((extent, 0), (1, extent + 1))):
+            region = [
+                pl.ds(0, dims[d] + 2) if d in done else pl.ds(1, dims[d]) for d in range(3)
+            ]
+            region[dim] = pl.ds(target, 1)
+            to = pad.at[tuple(region) + (slice(None), lanes)]
+            if stage == 0:
+                region = [pl.ds(0, dims[d]) for d in range(3)]
+                region[dim] = pl.ds(source - 1, 1)
+                come = block.at[tuple(region) + (slice(None), lanes)]
+            else:
+                region[dim] = pl.ds(source, 1)
+                come = pad.at[tuple(region) + (slice(None), lanes)]
+            copy = pltpu.make_async_remote_copy(
+                src_ref=come,
+                dst_ref=to,
+                send_sem=send_sem.at[stage, way, number],
+                recv_sem=recv_sem.at[stage, way, number],
+                device_id={axis: around[axis][way]},
+                device_id_type=MESH,
+            )
+            copy.start()
+            sent[stage, way, number] = copy
+
+    for number in range(len(units)):
+        send(0, number)
+    for copy in own:
+        copy.wait()
+    for stage in range(1, len(sides) + 1):
+        for number in range(len(units)):
+            for way in range(2):
+                sent[stage - 1, way, number].wait_recv()
+            if stage < len(sides):
+                send(stage, number)
+    for copy in sent.values():
+        copy.wait_send()
+
+
+def extended(blocks, identity):
+    dims = blocks[0].shape[:3]
+    vmem = pl.BlockSpec(memory_space=pltpu.VMEM)
+    count = sum(pieces if block.shape[-1] % (128 * pieces) == 0 else 1 for block in blocks)
+    return pl.pallas_call(
+        functools.partial(halo_kernel, len(blocks)),
+        out_shape=[
+            jax.ShapeDtypeStruct(tuple(d + 2 for d in dims) + block.shape[3:], block.dtype)
+            for block in blocks
+        ],
+        in_specs=[vmem] * len(blocks),
+        out_specs=[vmem] * len(blocks),
+        scratch_shapes=[
+            pltpu.SemaphoreType.DMA((len(blocks),)),
+            pltpu.SemaphoreType.DMA((len(sides), 2, count)),
+            pltpu.SemaphoreType.DMA((len(sides), 2, count)),
+        ],
+        compiler_params=pltpu.CompilerParams(collective_id=identity, has_side_effects=True),
+        name="halo",
+    )(*blocks)
+
+
+def total_kernel(axes, part, out, held, local_sem, send_sem, recv_sem):
+    barrier = pltpu.get_barrier_semaphore()
+    sizes = [lax.axis_size(axis) for axis in axes]
+    places = [lax.axis_index(axis) for axis in axes]
+    greeted = 0
+    for axis, size, me in zip(axes, sizes, places):
+        for step in range(1, size):
+            pl.semaphore_signal(
+                barrier, inc=1, device_id={axis: lax.rem(me + step, size)}, device_id_type=MESH
+            )
+            greeted += 1
+    own = pltpu.make_async_copy(part, held.at[places[2], places[1], places[0]], local_sem)
+    own.start()
+    pl.semaphore_wait(barrier, greeted)
+    own.wait()
+    for stage, (axis, size, me) in enumerate(zip(axes, sizes, places)):
+        if stage == 0:
+            view = held.at[places[2], places[1], places[0]]
+        elif stage == 1:
+            view = held.at[places[2], places[1]]
+        else:
+            view = held.at[places[2]]
+        copies = []
+        for step in range(1, size):
+            copy = pltpu.make_async_remote_copy(
+                src_ref=view,
+                dst_ref=view,
+                send_sem=send_sem.at[stage, step],
+                recv_sem=recv_sem.at[stage, step],
+                device_id={axis: lax.rem(me + step, size)},
+                device_id_type=MESH,
+            )
+            copy.start()
+            copies.append(copy)
+        for copy in copies:
+            copy.wait()
+    out[...] = jnp.sum(held[...], axis=(0, 1, 2))
+
+
+def summed(part, axes, identity):
+    sizes = [lax.axis_size(axis) for axis in axes]
+    vmem = pl.BlockSpec(memory_space=pltpu.VMEM)
+    return pl.pallas_call(
+        functools.partial(total_kernel, axes),
+        out_shape=jax.ShapeDtypeStruct(part.shape, part.dtype),
+        in_specs=[vmem],
+        out_specs=vmem,
+        scratch_shapes=[
+            pltpu.VMEM((sizes[2], sizes[1], sizes[0]) + part.shape, part.dtype),
+            pltpu.SemaphoreType.DMA,
+            pltpu.SemaphoreType.DMA((3, max(sizes))),
+            pltpu.SemaphoreType.DMA((3, max(sizes))),
+        ],
+        compiler_params=pltpu.CompilerParams(collective_id=identity, has_side_effects=True),
+        name="total",
+    )(part)
 
 
 def layer_kernel(
     grid_dims,
     max_chunks,
+    layer,
     counts,
+    ground,
+    feats,
+    radial_in_all,
+    radial_bias_all,
+    radial_out_all,
+    atom_in_all,
+    atom_bias_all,
+    atom_out_all,
+    readout_in,
+    readout_out,
+    out,
+    part_out,
     places,
-    feats,
     radial_block,
     radial_bias,
-    radial_out,
-    atom_in,
-    atom_bias,
-    atom_out,
-    out,
+    fresh,
     near_place,
     near_state,
     place_rows,
@@ -56,8 +209,29 @@
     pad_y, pad_z = deep + 2, tall + 2
     slots = feats.shape[1]
     width = feats.shape[2] // 4
-    hidden_width = radial_out.shape[0]
-    basis_count = radial_block.shape[1] // group
+    radial_out = radial_out_all.at[layer]
+    atom_out = atom_out_all.at[layer]
+    basis_count, hidden_width = radial_in_all.shape[1:]
+
+    @pl.when(cell == 0)
+    def _():
+        part_out[...] = jnp.zeros(part_out.shape, part_out.dtype)
+        small = 0.5 * radial_in_all[layer].astype(jnp.float32)
+        tall_form = jnp.concatenate([small] * group, axis=0)
+        wide_form = jnp.concatenate([tall_form] * (128 // hidden_width), axis=1).T[:hidden_width]
+        box = (group, hidden_width, group * basis_count)
+        spread = jnp.broadcast_to(wide_form[None], box)
+        owner = lax.div(lax.broadcasted_iota(jnp.int32, box, 2), basis_count)
+        spread = jnp.where(owner == lax.broadcasted_iota(jnp.int32, box, 0), spread, 0.0)
+        radial_block[...] = spread.reshape(radial_block.shape).astype(jnp.bfloat16)
+        bias = 0.5 * radial_bias_all[layer : layer + 1, :]
+        bias = jnp.concatenate([bias] * (128 // hidden_width), axis=1)
+        radial_bias[...] = jnp.broadcast_to(bias, (chunk, 128)).T[:hidden_width]
+
+        @pl.loop(0, ground.shape[0])
+        def _(index):
+            places[index, :, :8] = ground[index].T[:slots, :]
+
     lane = lax.broadcasted_iota(jnp.int32, (slots, width), 1)
 
     def cell_index(dx, dy, dz):
@@ -94,9 +268,9 @@
         place_rows[:, rows] = near_place[rows, :].T[:8, :]
         half = jnp.dot(
             near_state[0, rows, :].astype(jnp.bfloat16),
-            atom_in[...],
+            (0.5 * atom_in_all[layer].astype(jnp.float32)).astype(jnp.bfloat16),
             preferred_element_type=jnp.float32,
-        ) + atom_bias[...]
+        ) + 0.5 * atom_bias_all[layer : layer + 1, :]
         hidden = (half + half * jnp.tanh(half)).astype(jnp.bfloat16)
         gates = jnp.dot(hidden, atom_out[...], preferred_element_type=jnp.float32).astype(
             jnp.bfloat16
@@ -114,7 +288,7 @@
             turned_table[part, rows, width:] = (gate_g * vector).astype(jnp.bfloat16)
 
     own_count = counts[home]
-    out[0] = jnp.zeros(out.shape[1:], out.dtype)
+    fresh[...] = jnp.zeros(fresh.shape, fresh.dtype)
     sharpness = 0.5 * ((basis_count - 1) / cutoff) ** 2
 
     @pl.loop(0, lax.div(own_count + group - 1, group))
@@ -185,29 +359,46 @@
                 for part, change in enumerate([scalar] + vectors):
                     before = near_state[part, pl.ds(own_start + first, group), :]
                     after = jnp.where(alive, before + message_scale * change, 0.0)
-                    out[0, pl.ds(first, group), part * width : (part + 1) * width] = after
-
-
-def layer_update(cells_shape, counts, places, feats, params):
+                    fresh[pl.ds(first, group), part * width : (part + 1) * width] = after
+
+    rounded = fresh[...].astype(jnp.bfloat16)
+    out[0] = rounded
+    if layer == radial_in_all.shape[0] - 1:
+        read = jnp.dot(rounded[:, :width], readout_in[...], preferred_element_type=jnp.float32)
+        read = read / (1.0 + jnp.exp(-read)) * readout_out[...]
+        alive = lax.broadcasted_iota(jnp.int32, read.shape, 0) < own_count
+        amount = jnp.sum(jnp.where(alive, read, 0.0), axis=(0, 1), keepdims=True)
+        part_out[...] += jnp.broadcast_to(amount, part_out.shape)
+
+
+def layer_update(layer, cells_shape, counts, ground, feats, params):
     cells_wide, cells_deep, cells_tall = cells_shape
-    radial_in, radial_bias, radial_out, atom_in, atom_bias, atom_out = params
     total_cells = cells_wide * cells_deep * cells_tall
     slots = feats.shape[1]
     width = feats.shape[2] // 4
-    hidden_width = radial_in.shape[1]
+    basis_count, hidden_width = params[0].shape[1:]
     max_chunks = -(-27 * slots // chunk)
-    radial_block = jnp.kron(jnp.eye(group, dtype=jnp.float32), 0.5 * radial_in.astype(jnp.float32).T)
     span = max_chunks * chunk
     store = 27 * slots + chunk + slots
     store = -(-store // 8) * 8
     vmem = pl.BlockSpec(memory_space=pltpu.VMEM)
     return pl.pallas_call(
-        functools.partial(layer_kernel, (cells_deep, cells_tall), max_chunks),
+        functools.partial(layer_kernel, (cells_deep, cells_tall), max_chunks, layer),
         grid=(total_cells,),
-        out_shape=jax.ShapeDtypeStruct((total_cells, slots, 4 * width), jnp.float32),
-        in_specs=[pl.BlockSpec(memory_space=pltpu.SMEM)] + [vmem] * 8,
-        out_specs=pl.BlockSpec((1, slots, 4 * width), lambda i: (i, 0, 0)),
+        out_shape=(
+            jax.ShapeDtypeStruct((total_cells, slots, 4 * width), jnp.bfloat16),
+            jax.ShapeDtypeStruct((8, 128), jnp.float32),
+        ),
+        in_specs=[pl.BlockSpec(memory_space=pltpu.SMEM)] + [vmem] * (2 + len(params)),
+        out_specs=(
+            pl.BlockSpec((1, slots, 4 * width), lambda i: (i, 0, 0)),
+            pl.BlockSpec((8, 128), lambda i: (0, 0)),
+        ),
         scratch_shapes=[
+            pltpu.VMEM((ground.shape[0], slots, width), jnp.float32),
+            pltpu.VMEM((group * hidden_width, group * basis_count), jnp.bfloat16),
+            pltpu.VMEM((hidden_width, chunk), jnp.float32),
+            pltpu.VMEM((slots, 4 * width), jnp.float32),
             pltpu.VMEM((store, width), jnp.float32),
             pltpu.VMEM((4, store, width), jnp.float32),
             pltpu.VMEM((8, span), jnp.float32),
@@ -217,30 +408,7 @@
         ],
         compiler_params=pltpu.CompilerParams(vmem_limit_bytes=56 << 20),
         name="message_layer",
-    )(
-        counts,
-        places,
-        feats,
-        radial_block.astype(jnp.bfloat16),
-        jnp.broadcast_to(0.5 * radial_bias[:, None], (hidden_width, chunk)),
-        radial_out,
-        (0.5 * atom_in.astype(jnp.float32)).astype(jnp.bfloat16),
-        0.5 * atom_bias[None, :],
-        atom_out,
-    )
-
-
-def summed(value, axes):
-    for axis in axes:
-        count = lax.axis_size(axis)
-        if count & (count - 1):
-            value = lax.psum(value, axis)
-            continue
-        step = 1
-        while step < count:
-            value = value + lax.ppermute(value, axis, [(i, i ^ step) for i in range(count)])
-            step *= 2
-    return value
+    )(counts, ground, feats, *params)
 
 
 def on_device(
@@ -259,39 +427,36 @@
 ):
     cells_wide, cells_deep, cells_tall, slots, width = scalars.shape
     cells_shape = (cells_wide, cells_deep, cells_tall)
-    sides = (("gy", 1), ("gx", 0), ("gz", 2))
-    live = (
-        lax.broadcasted_iota(jnp.int32, cells_shape + (slots,), 3) < counts[:, :, :, None]
-    ).astype(jnp.float32)
     level = jnp.broadcast_to(counts.astype(jnp.float32)[..., None, None], cells_shape + (1, slots))
-    geometry = extended(jnp.concatenate([positions, level], axis=3), sides, 1)
-    near_counts = geometry[:, :, :, 3, 0].astype(jnp.int32).reshape(-1)
-    places = geometry.reshape((-1,) + geometry.shape[3:]).transpose(0, 2, 1)
-    places = jnp.pad(places, ((0, 0), (0, 0), (0, width - places.shape[2])))
+    geometry = jnp.concatenate([positions, level], axis=3)
+    geometry = jnp.pad(geometry, ((0, 0),) * 3 + ((0, 8 - geometry.shape[3]), (0, 128 - slots)))
     state = jnp.concatenate(
         [scalars, vectors.reshape(cells_shape + (slots, 3 * width))], axis=-1
     )
+    params = (
+        radial_in,
+        radial_bias,
+        radial_out,
+        atom_in,
+        atom_bias,
+        atom_out,
+        readout_in,
+        readout_out[None, :],
+    )
     for layer in range(radial_in.shape[0]):
-        params = (
-            radial_in[layer],
-            radial_bias[layer],
-            radial_out[layer],
-            atom_in[layer],
-            atom_bias[layer],
-            atom_out[layer],
+        if layer == 0:
+            feats, ground = extended([state, geometry], 0)
+            ground = ground.reshape((-1,) + ground.shape[3:])
+            near_counts = ground[:, 3, 0].astype(jnp.int32)
+        else:
+            (feats,) = extended([state], layer)
+        state, part = layer_update(
+            layer, cells_shape, near_counts, ground, feats.reshape(-1, slots, 4 * width), params
         )
-        feats = extended(state, sides, 1)
-        state = layer_update(
-            cells_shape, near_counts, places, feats.reshape(-1, slots, 4 * width), params
-        )
-        state = state.astype(jnp.bfloat16).reshape(cells_shape + (slots, 4 * width))
+        state = state.reshape(cells_shape + (slots, 4 * width))
     scalar_state = state[..., :width]
     vector_state = state[..., width:].reshape(cells_shape + (slots, 3, width))
-    readout_hidden = jax.nn.silu(
-        jnp.dot(scalar_state.reshape(-1, width), readout_in, preferred_element_type=jnp.float32)
-    )
-    atom_energy = jnp.sum(readout_hidden * readout_out, axis=-1) * live.reshape(-1)
-    energy = summed(jnp.sum(atom_energy).reshape(1), ("gx", "gy", "gz"))
+    energy = summed(part, ("gz", "gx", "gy"), radial_in.shape[0])[0, :1]
     return (scalar_state, vector_state, energy)
 
 

time: 121 us -> 106 us (0.88)
  Pallas kernels: 19.3 us -> 91.7 us
  starting transfers between devices: 46.1 us -> 0 us
  waiting for transfers between devices: 28.5 us -> 0 us
  local copies, waits for them, and re-layouts: 12.9 us -> 7.04 us
  between operations: 5.87 us -> 0.66 us
  other arithmetic: 7.29 us -> 4.77 us
    pallas_call x0 -> x3, Pallas kernels: none -> 66.3 us  [the longest x2 49.8 us: extended(): pl.pallas_call(functools.partial(halo_kernel, len(blocks)), out_shape=[ja...]
    ppermute x23 -> x0, starting transfers between devices: 46.1 us -> none  [the longest x5 17.6 us: summed(): lax.ppermute(value, axis, [(i, i ^ step) for i in range(count)])]
    ppermute x23 -> x0, waiting for transfers between devices: 28.5 us -> none  [the longest x9 14.5 us: extended(): lax.ppermute(lax.slice_in_dim(block, block.shape[dim] - width, None, axis...]
    pallas_call x2, Pallas kernels: 19.3 us -> 25.4 us  [layer_update(): pl.pallas_call(functools.partial(layer_kernel, (cells_deep, cells_tall),...]
    unnamed x18 -> x5, local copies, waits for them, and re-layouts: 1.55 us -> 4.91 us
    squeeze x2 -> x0, local copies, waits for them, and re-layouts: 3.2 us -> none  [the longest x1 1.68 us: on_device(): atom_out[layer]]
    concatenate x3 -> x0, local copies, waits for them, and re-layouts: 2.51 us -> none  [extended(): block = jnp.concatenate([low, block, high], axis=dim)]
    convert_element_type x5 -> x0, local copies, waits for them, and re-layouts: 2.39 us -> none  [the longest x4 1.78 us: layer_update(): radial_block.astype(jnp.bfloat16)]
  transfers between devices with their start and end apart: 23 -> 0, of which waited for: 14 -> 0; matrix products, arithmetic and copies ran while one was open for 10% -> 0% of each run, Pallas kernels for 0% -> 0%
where the time goes in v2:
time: 106 us; the launch traced here: 104 us
  Pallas kernels  91.7 us (87%)
  local copies, waits for them, and re-layouts  7.04 us (7%)
  other arithmetic  4.77 us (4%)
    pallas_call x2, Pallas kernels, extended(): pl.pallas_call(functools.partial(halo_kernel, len(blocks)), out_shape=[ja...  49.8 us
    pallas_call x2, Pallas kernels, layer_update(): pl.pallas_call(functools.partial(layer_kernel, (cells_deep, cells_tall),...  25.4 us
    pallas_call x1, Pallas kernels, summed(): pl.pallas_call(functools.partial(total_kernel, axes), out_shape=jax.Shape...  16.5 us
    unnamed x5, local copies, waits for them, and re-layouts  4.91 us
    convert_element_type x1, other arithmetic, on_device(): near_counts = ground[:, 3, 0].astype(jnp.int32)  2.16 us

profile of v2, /device:TPU:0, one launch (start us, length us, event | category | flops | bytes accessed | tf_op | source)
XLA Modules:
  0.0 104.2 jit_solution(2900807261358923124)
XLA Ops:
  0.6 0.8 copy.21
  1.5 0.1 reshape.31
  1.5 1.3 %pad_maximum_fusion.refs_0_ = bf16[2,1,1,32,512]{4,3,2,1,0:T(8,128)(2,1)} fusion(bf16[2,1,1,32,384]{4,3,2,1,0:T(8,128)(2,1)S(1)} %bitcast.23, bf16[2,1,1,32,128]{4,3,2,1,0:T(8,128)(2,1)} %param.14), kind=kLoop, calls=%fused_computation | loop fusion | flops 131072 | bytes 131072 | tf_op jit(solution)/shard_map/concatenate | solution.py:433
  2.9 0.7 copy.23
  3.6 0.7 convert_bitcast_fusion
  4.2 0.1 broadcast_in_dim.12
  4.3 0.6 select_maximum_fusion.refs_1_
  4.9 23.5 %halo.2 = (bf16[4,3,3,32,512]{4,3,2,1,0:T(8,128)(2,1)}, f32[4,3,3,8,128]{4,3,2,1,0:T(8,128)}) custom-call(bf16[2,1,1,32,512]{4,3,2,1,0:T(8,128)(2,1)} %pad_maximum_fusion.refs_0_, f32[2,1,1,8,128]{4,3,2,1,0:T(8,128)} %select_maximum_fusion.refs_1_), custom_call_target="tpu_custom_call" | custom-call | tf_op jit(solution)/shard_map/halo/pallas_call | solution.py:100
  28.4 2.2 %fusion.counts = s32[36]{0:T(128)} fusion(f32[36,8,128]{2,1,0:T(8,128)} %bitcast.20), kind=kLoop, calls=%fused_computation.2 | loop fusion | flops 36 | bytes 288 | tf_op jit(solution)/shard_map/convert_element_type | solution.py:450
  30.6 1.4 %copy.24.readout_in = bf16[128,64]{1,0:T(8,128)(2,1)} copy(bf16[128,64]{0,1:T(8,128)(2,1)} %param.22) | data formatting | bytes 32768 | tf_op args[10]
  32.0 12.4 %message_layer.2 = (bf16[2,32,512]{2,1,0:T(8,128)(2,1)}, f32[8,128]{1,0:T(8,128)}) custom-call(s32[36]{0:T(128)} %fusion.counts, f32[36,8,128]{2,1,0:T(8,128)} %bitcast.21, bf16[36,32,512]{2,1,0:T(8,128)(2,1)} %bitcast.19, bf16[2,8,64]{2,1,0:T(8,128)(2,1)} %radial_in_all.3, f32[2,64]{1,0:T(2,128)} %radial_bias_all.3, bf16[2,64,512]{2,1,0:T(8,128)(2,1)} %radial_out_all.3, ...), custom_call_target="tpu_custom_call" | custom-call | tf_op jit(solution)/shard_map/message_layer/pallas_call | solution.py:385
  44.4 26.2 %halo.3 = bf16[4,3,3,32,512]{4,3,2,1,0:T(8,128)(2,1)} custom-call(bf16[2,1,1,32,512]{4,3,2,1,0:T(8,128)(2,1)} %bitcast.24), custom_call_target="tpu_custom_call" | custom-call | tf_op jit(solution)/shard_map/halo/pallas_call | solution.py:100
  70.7 13.0 %message_layer.3 = (bf16[2,32,512]{2,1,0:T(8,128)(2,1)}, f32[8,128]{1,0:T(8,128)}) custom-call(s32[36]{0:T(128)} %fusion.counts, f32[36,8,128]{2,1,0:T(8,128)} %bitcast.22, bf16[36,32,512]{2,1,0:T(8,128)(2,1)} %bitcast.18, bf16[2,8,64]{2,1,0:T(8,128)(2,1)} %radial_in_all.3, f32[2,64]{1,0:T(2,128)} %radial_bias_all.3, bf16[2,64,512]{2,1,0:T(8,128)(2,1)} %radial_out_all.3, ...), custom_call_target="tpu_custom_call" | custom-call | tf_op jit(solution)/shard_map/message_layer/pallas_call | solution.py:385
  83.7 0.8 slice.18
  84.5 0.6 copy.27
  85.2 1.3 %slice_bitcast_fusion = bf16[2,1,1,32,128]{4,3,2,1,0:T(8,128)(2,1)} fusion(bf16[2,1,1,32,512]{4,3,0,2,1:T(8,128)(2,1)} %bitcast.26), kind=kLoop, calls=%fused_computation.3 | loop fusion | bytes 32768
  86.5 16.5 %total.1 = f32[8,128]{1,0:T(8,128)} custom-call(f32[8,128]{1,0:T(8,128)} %get-tuple-element.12.part), custom_call_target="tpu_custom_call" | custom-call | tf_op jit(solution)/shard_map/total/pallas_call | solution.py:160
  103.0 1.2 %slice.15 = f32[1,1]{1,0:T(1,128)} slice(f32[8,128]{1,0:T(8,128)} %total.1), slice={[0:1], [0:1]} | slice | bytes 8 | tf_op jit(solution)/shard_map/slice | solution.py:459
  (1 shorter events, 0.0 us)

commit v3 on v2

--- a/solution.py
+++ b/solution.py
@@ -25,10 +25,39 @@
     return lax.rem(me + 1, count), lax.rem(me + count - 1, count)
 
 
-def halo_kernel(array_count, *refs):
-    blocks = refs[:array_count]
-    pads = refs[array_count : 2 * array_count]
-    local_sem, send_sem, recv_sem = refs[2 * array_count :]
+def prepare(ground, radial_in, radial_bias, places, counts, radial_block, bias_wide):
+    wide, deep, tall = ground.shape[:3]
+    slots = places.shape[1]
+    layers, basis_count, hidden_width = radial_in.shape
+    for x in range(wide):
+        for y in range(deep):
+            for z in range(tall):
+                index = (x * deep + y) * tall + z
+                tile = ground[x, y, z]
+                places[index, :, :8] = tile.T[:slots, :]
+                counts[index : index + 1, :] = tile[3:4, :].astype(jnp.int32)
+    box = (group, hidden_width, group * basis_count)
+    owner = lax.div(lax.broadcasted_iota(jnp.int32, box, 2), basis_count)
+    match = owner == lax.broadcasted_iota(jnp.int32, box, 0)
+    for layer in range(layers):
+        small = 0.5 * radial_in[layer].astype(jnp.float32)
+        tall_form = jnp.concatenate([small] * group, axis=0)
+        wide_form = jnp.concatenate([tall_form] * (128 // hidden_width), axis=1).T[:hidden_width]
+        spread = jnp.where(match, jnp.broadcast_to(wide_form[None], box), 0.0)
+        radial_block[layer] = spread.reshape(radial_block.shape[1:]).astype(jnp.bfloat16)
+        bias = 0.5 * radial_bias[layer : layer + 1, :]
+        bias = jnp.concatenate([bias] * (128 // hidden_width), axis=1)
+        bias_wide[layer] = jnp.broadcast_to(bias, (chunk, 128)).T[:hidden_width]
+
+
+def halo_kernel(first, *refs):
+    if first:
+        state, geometry, radial_in, radial_bias, feats, *made = refs[:9]
+        ground, local_sem, send_sem, recv_sem = refs[9:]
+        blocks, pads = [state, geometry], [feats, ground]
+    else:
+        state, feats, local_sem, send_sem, recv_sem = refs
+        blocks, pads = [state], [feats]
     dims = blocks[0].shape[:3]
     around = {axis: ring(axis) for axis, _ in sides}
     barrier = pltpu.get_barrier_semaphore()
@@ -41,7 +70,7 @@
         cuts = pieces if lanes % (128 * pieces) == 0 else 1
         for cut in range(cuts):
             units.append((block, pad, pl.ds(cut * (lanes // cuts), lanes // cuts)))
-    units = units[::-1] if array_count > 1 else units
+    units = units[::-1]
     center = tuple(pl.ds(1, extent) for extent in dims)
     own = []
     for place, (block, pad) in enumerate(zip(blocks, pads)):
@@ -89,30 +118,46 @@
                 sent[stage - 1, way, number].wait_recv()
             if stage < len(sides):
                 send(stage, number)
+            elif number == 0 and first:
+                prepare(ground, radial_in, radial_bias, *made)
     for copy in sent.values():
         copy.wait_send()
 
 
-def extended(blocks, identity):
-    dims = blocks[0].shape[:3]
+def extended(state, identity, extra=()):
+    dims = state.shape[:3]
+    slots = state.shape[3]
     vmem = pl.BlockSpec(memory_space=pltpu.VMEM)
-    count = sum(pieces if block.shape[-1] % (128 * pieces) == 0 else 1 for block in blocks)
+    outer = tuple(d + 2 for d in dims)
+    cells = math.prod(outer)
+    shapes = [jax.ShapeDtypeStruct(outer + state.shape[3:], state.dtype)]
+    scratch = []
+    units = pieces if state.shape[-1] % (128 * pieces) == 0 else 1
+    if extra:
+        layers, basis_count, hidden_width = extra[1].shape
+        rows = group * hidden_width
+        shapes += [
+            jax.ShapeDtypeStruct((cells, slots, 128), jnp.float32),
+            jax.ShapeDtypeStruct((cells, 128), jnp.int32),
+            jax.ShapeDtypeStruct((layers, rows, group * basis_count), jnp.bfloat16),
+            jax.ShapeDtypeStruct((layers, hidden_width, chunk), jnp.float32),
+        ]
+        scratch = [pltpu.VMEM(outer + extra[0].shape[3:], extra[0].dtype)]
+        units += 1
     return pl.pallas_call(
-        functools.partial(halo_kernel, len(blocks)),
-        out_shape=[
-            jax.ShapeDtypeStruct(tuple(d + 2 for d in dims) + block.shape[3:], block.dtype)
-            for block in blocks
-        ],
-        in_specs=[vmem] * len(blocks),
-        out_specs=[vmem] * len(blocks),
-        scratch_shapes=[
-            pltpu.SemaphoreType.DMA((len(blocks),)),
-            pltpu.SemaphoreType.DMA((len(sides), 2, count)),
-            pltpu.SemaphoreType.DMA((len(sides), 2, count)),
+        functools.partial(halo_kernel, bool(extra)),
+        out_shape=shapes,
+        in_specs=[vmem] * (1 + len(extra)),
+        out_specs=[vmem] * len(shapes),
+        scratch_shapes=scratch
+        + [
+            pltpu.SemaphoreType.DMA((2,)),
+            pltpu.SemaphoreType.DMA((len(sides), 2, units)),
+            pltpu.SemaphoreType.DMA((len(sides), 2, units)),
         ],
         compiler_params=pltpu.CompilerParams(collective_id=identity, has_side_effects=True),
         name="halo",
-    )(*blocks)
+    )(state, *extra)
 
 
 def total_kernel(axes, part, out, held, local_sem, send_sem, recv_sem):
@@ -151,7 +196,7 @@
             copies.append(copy)
         for copy in copies:
             copy.wait()
-    out[...] = jnp.sum(held[...], axis=(0, 1, 2))
+    out[0] = jnp.sum(held[...]) / (part.shape[0] * part.shape[1])
 
 
 def summed(part, axes, identity):
@@ -159,9 +204,9 @@
     vmem = pl.BlockSpec(memory_space=pltpu.VMEM)
     return pl.pallas_call(
         functools.partial(total_kernel, axes),
-        out_shape=jax.ShapeDtypeStruct(part.shape, part.dtype),
+        out_shape=jax.ShapeDtypeStruct((1,), part.dtype),
         in_specs=[vmem],
-        out_specs=vmem,
+        out_specs=pl.BlockSpec(memory_space=pltpu.SMEM),
         scratch_shapes=[
             pltpu.VMEM((sizes[2], sizes[1], sizes[0]) + part.shape, part.dtype),
             pltpu.SemaphoreType.DMA,
@@ -178,10 +223,10 @@
     max_chunks,
     layer,
     counts,
-    ground,
+    places,
     feats,
-    radial_in_all,
-    radial_bias_all,
+    radial_blocks,
+    bias_wide,
     radial_out_all,
     atom_in_all,
     atom_bias_all,
@@ -190,13 +235,10 @@
     readout_out,
     out,
     part_out,
-    places,
-    radial_block,
-    radial_bias,
     fresh,
+    spots,
     near_place,
     near_state,
-    place_rows,
     edges,
     plain_table,
     turned_table,
@@ -211,26 +253,12 @@
     width = feats.shape[2] // 4
     radial_out = radial_out_all.at[layer]
     atom_out = atom_out_all.at[layer]
-    basis_count, hidden_width = radial_in_all.shape[1:]
+    hidden_width = radial_out.shape[0]
+    basis_count = radial_blocks.shape[2] // group
 
     @pl.when(cell == 0)
     def _():
         part_out[...] = jnp.zeros(part_out.shape, part_out.dtype)
-        small = 0.5 * radial_in_all[layer].astype(jnp.float32)
-        tall_form = jnp.concatenate([small] * group, axis=0)
-        wide_form = jnp.concatenate([tall_form] * (128 // hidden_width), axis=1).T[:hidden_width]
-        box = (group, hidden_width, group * basis_count)
-        spread = jnp.broadcast_to(wide_form[None], box)
-        owner = lax.div(lax.broadcasted_iota(jnp.int32, box, 2), basis_count)
-        spread = jnp.where(owner == lax.broadcasted_iota(jnp.int32, box, 0), spread, 0.0)
-        radial_block[...] = spread.reshape(radial_block.shape).astype(jnp.bfloat16)
-        bias = 0.5 * radial_bias_all[layer : layer + 1, :]
-        bias = jnp.concatenate([bias] * (128 // hidden_width), axis=1)
-        radial_bias[...] = jnp.broadcast_to(bias, (chunk, 128)).T[:hidden_width]
-
-        @pl.loop(0, ground.shape[0])
-        def _(index):
-            places[index, :, :8] = ground[index].T[:slots, :]
 
     lane = lax.broadcasted_iota(jnp.int32, (slots, width), 1)
 
@@ -255,7 +283,7 @@
                     near_state[part, pl.ds(total, slots), :] = block[
                         :, part * width : (part + 1) * width
                     ]
-                total = total + counts[index]
+                total = total + counts[index, 0]
     blank = jnp.zeros((chunk, width), jnp.float32)
     near_place[pl.ds(total, chunk), :] = blank
     for part in range(4):
@@ -265,7 +293,22 @@
     @pl.loop(0, chunks)
     def _(step):
         rows = pl.ds(pl.multiple_of(step * chunk, chunk), chunk)
-        place_rows[:, rows] = near_place[rows, :].T[:8, :]
+        near = near_place[rows, :].T[:8, :]
+        mine = places[home]
+        col = step * chunk + lax.broadcasted_iota(jnp.int32, (slots, chunk), 1)
+        row = lax.broadcasted_iota(jnp.int32, (slots, chunk), 0)
+        unused = jnp.logical_or(col == own_start + row, col >= total)
+        offset = [near[k : k + 1, :] - mine[:, k : k + 1] for k in range(3)]
+        square = offset[0] * offset[0] + offset[1] * offset[1] + offset[2] * offset[2]
+        distance = jnp.sqrt(square + jnp.where(unused, 1.0, 0.0))
+        inverse = 1.0 / distance
+        smooth = 0.5 * (jnp.cos(math.pi / cutoff * distance) + 1.0)
+        spots[0, :, rows] = distance
+        spots[1, :, rows] = jnp.where(
+            jnp.logical_and(distance < cutoff, jnp.logical_not(unused)), smooth, 0.0
+        )
+        for k in range(3):
+            spots[k + 2, :, rows] = offset[k] * inverse
         half = jnp.dot(
             near_state[0, rows, :].astype(jnp.bfloat16),
             (0.5 * atom_in_all[layer].astype(jnp.float32)).astype(jnp.bfloat16),
@@ -287,41 +330,32 @@
             turned_table[part, rows, :width] = gate_c
             turned_table[part, rows, width:] = (gate_g * vector).astype(jnp.bfloat16)
 
-    own_count = counts[home]
+    own_count = counts[home, 0]
     fresh[...] = jnp.zeros(fresh.shape, fresh.dtype)
     sharpness = 0.5 * ((basis_count - 1) / cutoff) ** 2
 
     @pl.loop(0, lax.div(own_count + group - 1, group))
     def _(turn):
         first = pl.multiple_of(turn * group, group)
-        mine = places[home, pl.ds(first, group), :]
-
-        @pl.loop(0, chunks)
-        def _(step):
-            columns = pl.ds(pl.multiple_of(step * chunk, chunk), chunk)
-            col = step * chunk + lax.broadcasted_iota(jnp.int32, (group, chunk), 1)
-            row = first + lax.broadcasted_iota(jnp.int32, (group, chunk), 0)
-            unused = jnp.logical_or(col == own_start + row, col >= total)
-            offset = [place_rows[k : k + 1, columns] - mine[:, k : k + 1] for k in range(3)]
-            square = offset[0] * offset[0] + offset[1] * offset[1] + offset[2] * offset[2]
-            distance = jnp.sqrt(square + jnp.where(unused, 1.0, 0.0))
-            inverse = 1.0 / distance
-            smooth = 0.5 * (jnp.cos(math.pi / cutoff * distance) + 1.0)
-            weight = jnp.where(
-                jnp.logical_and(distance < cutoff, jnp.logical_not(unused)), smooth, 0.0
-            )
+
+        def form_edges(step):
+            columns = slice(step * chunk, (step + 1) * chunk)
+            receivers = pl.ds(first, group)
+            distance = spots[0, receivers, columns]
             centers = lax.broadcasted_iota(jnp.int32, (1, basis_count, chunk), 1).astype(
                 jnp.float32
             ) * (cutoff / (basis_count - 1))
             gap = distance[:, None, :] - centers
             basis = jnp.exp(-sharpness * gap * gap).reshape(group * basis_count, chunk)
             half = jnp.dot(
-                radial_block[...], basis.astype(jnp.bfloat16), preferred_element_type=jnp.float32
-            ).reshape(group, hidden_width, chunk) + radial_bias[...][None]
-            active = (half + half * jnp.tanh(half)) * weight[:, None, :]
+                radial_blocks[layer],
+                basis.astype(jnp.bfloat16),
+                preferred_element_type=jnp.float32,
+            ).reshape(group, hidden_width, chunk) + bias_wide[layer][None]
+            active = (half + half * jnp.tanh(half)) * spots[1, receivers, columns][:, None, :]
             edges[0, :, columns] = active.reshape(group * hidden_width, chunk).astype(jnp.bfloat16)
             for k in range(3):
-                unit = (offset[k] * inverse)[:, None, :]
+                unit = spots[k + 2, receivers, columns][:, None, :]
                 edges[k + 1, :, columns] = (
                     (active * unit).reshape(group * hidden_width, chunk).astype(jnp.bfloat16)
                 )
@@ -331,6 +365,8 @@
             @pl.when(chunks == used)
             def _(used=used):
                 span = used * chunk
+                for step in range(used):
+                    form_edges(step)
 
                 def contracted(left, right, filters):
                     product = jnp.dot(left, right, preferred_element_type=jnp.float32)
@@ -363,20 +399,25 @@
 
     rounded = fresh[...].astype(jnp.bfloat16)
     out[0] = rounded
-    if layer == radial_in_all.shape[0] - 1:
-        read = jnp.dot(rounded[:, :width], readout_in[...], preferred_element_type=jnp.float32)
+    if layer == radial_out_all.shape[0] - 1:
+        read = lax.dot_general(
+            rounded[:, :width],
+            readout_in[...],
+            (((1,), (1,)), ((), ())),
+            preferred_element_type=jnp.float32,
+        )
         read = read / (1.0 + jnp.exp(-read)) * readout_out[...]
         alive = lax.broadcasted_iota(jnp.int32, read.shape, 0) < own_count
         amount = jnp.sum(jnp.where(alive, read, 0.0), axis=(0, 1), keepdims=True)
         part_out[...] += jnp.broadcast_to(amount, part_out.shape)
 
 
-def layer_update(layer, cells_shape, counts, ground, feats, params):
+def layer_update(layer, cells_shape, counts, places, feats, params):
     cells_wide, cells_deep, cells_tall = cells_shape
     total_cells = cells_wide * cells_deep * cells_tall
     slots = feats.shape[1]
     width = feats.shape[2] // 4
-    basis_count, hidden_width = params[0].shape[1:]
+    hidden_width = params[1].shape[1]
     max_chunks = -(-27 * slots // chunk)
     span = max_chunks * chunk
     store = 27 * slots + chunk + slots
@@ -395,20 +436,17 @@
             pl.BlockSpec((8, 128), lambda i: (0, 0)),
         ),
         scratch_shapes=[
-            pltpu.VMEM((ground.shape[0], slots, width), jnp.float32),
-            pltpu.VMEM((group * hidden_width, group * basis_count), jnp.bfloat16),
-            pltpu.VMEM((hidden_width, chunk), jnp.float32),
             pltpu.VMEM((slots, 4 * width), jnp.float32),
+            pltpu.VMEM((5, slots, span), jnp.float32),
             pltpu.VMEM((store, width), jnp.float32),
             pltpu.VMEM((4, store, width), jnp.float32),
-            pltpu.VMEM((8, span), jnp.float32),
             pltpu.VMEM((4, group * hidden_width, span), jnp.bfloat16),
             pltpu.VMEM((span, 4 * width), jnp.bfloat16),
             pltpu.VMEM((3, span, 2 * width), jnp.bfloat16),
         ],
         compiler_params=pltpu.CompilerParams(vmem_limit_bytes=56 << 20),
         name="message_layer",
-    )(counts, ground, feats, *params)
+    )(counts, places, feats, *params)
 
 
 def on_device(
@@ -433,30 +471,22 @@
     state = jnp.concatenate(
         [scalars, vectors.reshape(cells_shape + (slots, 3 * width))], axis=-1
     )
-    params = (
-        radial_in,
-        radial_bias,
-        radial_out,
-        atom_in,
-        atom_bias,
-        atom_out,
-        readout_in,
-        readout_out[None, :],
-    )
+    params = (radial_out, atom_in, atom_bias, atom_out, readout_in.T, readout_out[None, :])
     for layer in range(radial_in.shape[0]):
         if layer == 0:
-            feats, ground = extended([state, geometry], 0)
-            ground = ground.reshape((-1,) + ground.shape[3:])
-            near_counts = ground[:, 3, 0].astype(jnp.int32)
+            feats, places, near_counts, blocks, bias_wide = extended(
+                state, 0, (geometry, radial_in, radial_bias)
+            )
+            params = (blocks, bias_wide) + params
         else:
-            (feats,) = extended([state], layer)
+            (feats,) = extended(state, layer)
         state, part = layer_update(
-            layer, cells_shape, near_counts, ground, feats.reshape(-1, slots, 4 * width), params
+            layer, cells_shape, near_counts, places, feats.reshape(-1, slots, 4 * width), params
         )
         state = state.reshape(cells_shape + (slots, 4 * width))
     scalar_state = state[..., :width]
     vector_state = state[..., width:].reshape(cells_shape + (slots, 3, width))
-    energy = summed(part, ("gz", "gx", "gy"), radial_in.shape[0])[0, :1]
+    energy = summed(part, ("gz", "gx", "gy"), radial_in.shape[0])
     return (scalar_state, vector_state, energy)
 
 

time: 106 us -> 94.7 us (0.89); the launches traced: 104 us -> 94 us
  Pallas kernels: 91.7 us -> 84.5 us
  local copies, waits for them, and re-layouts: 7.04 us -> 4.42 us
  other arithmetic: 4.77 us -> 2.62 us
  between operations: 0.66 us -> 2.43 us
    pallas_call x2, Pallas kernels: 25.4 us -> 15.9 us  [layer_update(): pl.pallas_call(functools.partial(layer_kernel, (cells_deep, cells_tall),...]
    pallas_call x1, Pallas kernels: 16.5 us -> 20.8 us  [summed(): pl.pallas_call(functools.partial(total_kernel, axes), out_shape=jax.Shape...]
    convert_element_type x1 -> x0, other arithmetic: 2.16 us -> none  [on_device(): near_counts = ground[:, 3, 0].astype(jnp.int32)]
    pallas_call x2, Pallas kernels: 49.8 us -> 47.8 us  [extended(): pl.pallas_call(functools.partial(halo_kernel, bool(extra)), out_shape=sha...]
    unnamed x5 -> x4, local copies, waits for them, and re-layouts: 4.91 us -> 3.47 us
    slice x1 -> x0, local copies, waits for them, and re-layouts: 1.18 us -> none  [on_device(): energy = summed(part, ('gz', 'gx', 'gy'), radial_in.shape[0])[0, :1]]
where the time goes in v3:
time: 94.7 us; the launch traced here: 94 us
  Pallas kernels  84.5 us (89%)
  local copies, waits for them, and re-layouts  4.42 us (5%)
  other arithmetic  2.62 us (3%)
  between operations  2.43 us (3%)
    pallas_call x2, Pallas kernels, extended(): pl.pallas_call(functools.partial(halo_kernel, bool(extra)), out_shape=sha...  47.8 us
    pallas_call x1, Pallas kernels, summed(): pl.pallas_call(functools.partial(total_kernel, axes), out_shape=jax.Shape...  20.8 us
    pallas_call x2, Pallas kernels, layer_update(): pl.pallas_call(functools.partial(layer_kernel, (cells_deep, cells_tall),...  15.9 us
    unnamed x4, local copies, waits for them, and re-layouts  3.47 us

profile of v3, /device:TPU:0, one launch (start us, length us, event | category | flops | bytes accessed | tf_op | source)
XLA Modules:
  0.0 94.0 jit_solution(4271106582986962898)
XLA Ops:
  0.6 0.7 convert_bitcast_fusion
  1.3 0.1 broadcast_in_dim.12
  1.4 0.7 copy.21
  2.0 0.6 select_maximum_fusion.refs_1_
  2.7 0.8 copy.19
  3.5 0.1 reshape.27
  3.5 1.4 %pad_maximum_fusion.refs_0_ = bf16[2,1,1,32,512]{4,3,2,1,0:T(8,128)(2,1)} fusion(bf16[2,1,1,32,384]{4,3,2,1,0:T(8,128)(2,1)S(1)} %bitcast.19, bf16[2,1,1,32,128]{4,3,2,1,0:T(8,128)(2,1)} %param.14), kind=kLoop, calls=%fused_computation | loop fusion | flops 131072 | bytes 131072 | tf_op jit(solution)/shard_map/concatenate | solution.py:471
  4.9 23.8 %halo.2 = (bf16[4,3,3,32,512]{4,3,2,1,0:T(8,128)(2,1)}, f32[36,32,128]{2,1,0:T(8,128)}, s32[36,128]{1,0:T(8,128)}, bf16[2,512,64]{2,1,0:T(8,128)(2,1)}, f32[2,64,256]{2,1,0:T(8,128)}) custom-call(bf16[2,1,1,32,512]{4,3,2,1,0:T(8,128)(2,1)} %pad_maximum_fusion.refs_0_, f32[2,1,1,8,128]{4,3,2,1,0:T(8,128)} %select_maximum_fusion.refs_1_, ...), custom_call_target="tpu_custom_call" | custom-call | tf_op jit(solution)/shard_map/halo/pallas_call | solution.py:147
  28.7 7.6 %message_layer.2 = (bf16[2,32,512]{2,1,0:T(8,128)(2,1)}, f32[8,128]{1,0:T(8,128)}) custom-call(s32[36,128]{1,0:T(8,128)} %get-tuple-element.11.counts, f32[36,32,128]{2,1,0:T(8,128)} %get-tuple-element.12.places, bf16[36,32,512]{2,1,0:T(8,128)(2,1)} %bitcast.18, bf16[2,512,64]{2,1,0:T(8,128)(2,1)} %get-tuple-element.14.radial_blocks, ...), custom_call_target="tpu_custom_call" | custom-call | tf_op jit(solution)/shard_map/message_layer/pallas_call | solution.py:426
  36.3 24.0 %halo.3 = bf16[4,3,3,32,512]{4,3,2,1,0:T(8,128)(2,1)} custom-call(bf16[2,1,1,32,512]{4,3,2,1,0:T(8,128)(2,1)} %bitcast.22), custom_call_target="tpu_custom_call" | custom-call | tf_op jit(solution)/shard_map/halo/pallas_call | solution.py:147
  60.3 8.3 %message_layer.3 = (bf16[2,32,512]{2,1,0:T(8,128)(2,1)}, f32[8,128]{1,0:T(8,128)}) custom-call(s32[36,128]{1,0:T(8,128)} %get-tuple-element.11.counts, f32[36,32,128]{2,1,0:T(8,128)} %get-tuple-element.12.places, bf16[36,32,512]{2,1,0:T(8,128)(2,1)} %bitcast.17, bf16[2,512,64]{2,1,0:T(8,128)(2,1)} %get-tuple-element.14.radial_blocks, ...), custom_call_target="tpu_custom_call" | custom-call | tf_op jit(solution)/shard_map/message_layer/pallas_call | solution.py:426
  68.6 20.8 %total.1 = f32[1]{0:T(128)} custom-call(f32[8,128]{1,0:T(8,128)} %get-tuple-element.18.part), custom_call_target="tpu_custom_call" | custom-call | tf_op jit(solution)/shard_map/total/pallas_call | solution.py:205
  89.5 1.3 %slice_bitcast_fusion = bf16[2,1,1,32,128]{4,3,2,1,0:T(8,128)(2,1)} fusion(bf16[2,1,1,32,512]{4,3,0,2,1:T(8,128)(2,1)} %bitcast.23), kind=kLoop, calls=%fused_computation.1 | loop fusion | bytes 32768
  90.8 0.8 slice.9
  91.6 0.6 copy.23
  (1 shorter events, 0.0 us)

commit v4 on v3

--- a/solution.py
+++ b/solution.py
@@ -15,8 +15,8 @@
 
 
 MESH = pl.DeviceIdType.MESH
-pieces = 4
 sides = (("gy", 1), ("gx", 0), ("gz", 2))
+other_sides = (("gy", 1), ("gz", 2), ("gx", 0))
 
 
 def ring(axis):
@@ -33,7 +33,7 @@
         for y in range(deep):
             for z in range(tall):
                 index = (x * deep + y) * tall + z
-                tile = ground[x, y, z]
+                tile = ground[x, y, z, 0]
                 places[index, :, :8] = tile.T[:slots, :]
                 counts[index : index + 1, :] = tile[3:4, :].astype(jnp.int32)
     box = (group, hidden_width, group * basis_count)
@@ -52,12 +52,13 @@
 
 def halo_kernel(first, *refs):
     if first:
-        state, geometry, radial_in, radial_bias, feats, *made = refs[:9]
-        ground, local_sem, send_sem, recv_sem = refs[9:]
-        blocks, pads = [state, geometry], [feats, ground]
+        blocks, (radial_in, radial_bias) = refs[:3], refs[3:5]
+        made = refs[7:11]
+        ground, local_sem, send_sem, recv_sem = refs[11:]
+        pads = refs[5:7] + (ground,)
     else:
-        state, feats, local_sem, send_sem, recv_sem = refs
-        blocks, pads = [state], [feats]
+        blocks, pads = refs[:2], refs[2:4]
+        local_sem, send_sem, recv_sem = refs[4:]
     dims = blocks[0].shape[:3]
     around = {axis: ring(axis) for axis, _ in sides}
     barrier = pltpu.get_barrier_semaphore()
@@ -66,11 +67,10 @@
             pl.semaphore_signal(barrier, inc=1, device_id={axis: side}, device_id_type=MESH)
     units = []
     for block, pad in zip(blocks, pads):
-        lanes = block.shape[-1]
-        cuts = pieces if lanes % (128 * pieces) == 0 else 1
-        for cut in range(cuts):
-            units.append((block, pad, pl.ds(cut * (lanes // cuts), lanes // cuts)))
+        for part in range(block.shape[3]):
+            units.append((block, pad, pl.ds(part, 1), sides))
     units = units[::-1]
+    units[-1] = units[-1][:3] + (other_sides,)
     center = tuple(pl.ds(1, extent) for extent in dims)
     own = []
     for place, (block, pad) in enumerate(zip(blocks, pads)):
@@ -80,23 +80,23 @@
     sent = {}
 
     def send(stage, number):
-        block, pad, lanes = units[number]
-        axis, dim = sides[stage]
-        done = [d for _, d in sides[:stage]]
+        block, pad, part, order = units[number]
+        axis, dim = order[stage]
+        done = [d for _, d in order[:stage]]
         extent = dims[dim]
         for way, (source, target) in enumerate(((extent, 0), (1, extent + 1))):
             region = [
                 pl.ds(0, dims[d] + 2) if d in done else pl.ds(1, dims[d]) for d in range(3)
             ]
             region[dim] = pl.ds(target, 1)
-            to = pad.at[tuple(region) + (slice(None), lanes)]
+            to = pad.at[tuple(region) + (part,)]
             if stage == 0:
                 region = [pl.ds(0, dims[d]) for d in range(3)]
                 region[dim] = pl.ds(source - 1, 1)
-                come = block.at[tuple(region) + (slice(None), lanes)]
+                come = block.at[tuple(region) + (part,)]
             else:
                 region[dim] = pl.ds(source, 1)
-                come = pad.at[tuple(region) + (slice(None), lanes)]
+                come = pad.at[tuple(region) + (part,)]
             copy = pltpu.make_async_remote_copy(
                 src_ref=come,
                 dst_ref=to,
@@ -124,15 +124,15 @@
         copy.wait_send()
 
 
-def extended(state, identity, extra=()):
-    dims = state.shape[:3]
-    slots = state.shape[3]
+def extended(states, identity, extra=()):
+    dims = states[0].shape[:3]
+    slots = states[0].shape[4]
     vmem = pl.BlockSpec(memory_space=pltpu.VMEM)
     outer = tuple(d + 2 for d in dims)
     cells = math.prod(outer)
-    shapes = [jax.ShapeDtypeStruct(outer + state.shape[3:], state.dtype)]
+    shapes = [jax.ShapeDtypeStruct(outer + state.shape[3:], state.dtype) for state in states]
     scratch = []
-    units = pieces if state.shape[-1] % (128 * pieces) == 0 else 1
+    units = sum(state.shape[3] for state in states)
     if extra:
         layers, basis_count, hidden_width = extra[1].shape
         rows = group * hidden_width
@@ -147,17 +147,17 @@
     return pl.pallas_call(
         functools.partial(halo_kernel, bool(extra)),
         out_shape=shapes,
-        in_specs=[vmem] * (1 + len(extra)),
+        in_specs=[vmem] * (len(states) + len(extra)),
         out_specs=[vmem] * len(shapes),
         scratch_shapes=scratch
         + [
-            pltpu.SemaphoreType.DMA((2,)),
+            pltpu.SemaphoreType.DMA((3,)),
             pltpu.SemaphoreType.DMA((len(sides), 2, units)),
             pltpu.SemaphoreType.DMA((len(sides), 2, units)),
         ],
         compiler_params=pltpu.CompilerParams(collective_id=identity, has_side_effects=True),
         name="halo",
-    )(state, *extra)
+    )(*states, *extra)
 
 
 def total_kernel(axes, part, out, held, local_sem, send_sem, recv_sem):
@@ -224,7 +224,8 @@
     layer,
     counts,
     places,
-    feats,
+    near_scalars,
+    near_vectors,
     radial_blocks,
     bias_wide,
     radial_out_all,
@@ -233,7 +234,8 @@
     atom_out_all,
     readout_in,
     readout_out,
-    out,
+    scalars_out,
+    vectors_out,
     part_out,
     fresh,
     spots,
@@ -249,8 +251,7 @@
     at_y = lax.rem(lax.div(cell, tall), deep)
     at_z = lax.rem(cell, tall)
     pad_y, pad_z = deep + 2, tall + 2
-    slots = feats.shape[1]
-    width = feats.shape[2] // 4
+    slots, width = near_scalars.shape[2:]
     radial_out = radial_out_all.at[layer]
     atom_out = atom_out_all.at[layer]
     hidden_width = radial_out.shape[0]
@@ -278,11 +279,11 @@
                     lane == 0, float(dx - 1), jnp.where(lane == 1, float(dy - 1), float(dz - 1))
                 )
                 near_place[pl.ds(total, slots), :] = places[index] + shift * cutoff
-                block = feats[index].astype(jnp.float32)
-                for part in range(4):
-                    near_state[part, pl.ds(total, slots), :] = block[
-                        :, part * width : (part + 1) * width
-                    ]
+                near_state[0, pl.ds(total, slots), :] = near_scalars[index, 0].astype(jnp.float32)
+                for part in range(3):
+                    near_state[part + 1, pl.ds(total, slots), :] = near_vectors[
+                        index, part
+                    ].astype(jnp.float32)
                 total = total + counts[index, 0]
     blank = jnp.zeros((chunk, width), jnp.float32)
     near_place[pl.ds(total, chunk), :] = blank
@@ -398,7 +399,9 @@
                     fresh[pl.ds(first, group), part * width : (part + 1) * width] = after
 
     rounded = fresh[...].astype(jnp.bfloat16)
-    out[0] = rounded
+    scalars_out[0, 0] = rounded[:, :width]
+    for part in range(3):
+        vectors_out[0, part] = rounded[:, (part + 1) * width : (part + 2) * width]
     if layer == radial_out_all.shape[0] - 1:
         read = lax.dot_general(
             rounded[:, :width],
@@ -412,11 +415,11 @@
         part_out[...] += jnp.broadcast_to(amount, part_out.shape)
 
 
-def layer_update(layer, cells_shape, counts, places, feats, params):
+def layer_update(layer, cells_shape, counts, places, states, params):
     cells_wide, cells_deep, cells_tall = cells_shape
     total_cells = cells_wide * cells_deep * cells_tall
-    slots = feats.shape[1]
-    width = feats.shape[2] // 4
+    states = [state.reshape((-1,) + state.shape[3:]) for state in states]
+    slots, width = states[0].shape[2:]
     hidden_width = params[1].shape[1]
     max_chunks = -(-27 * slots // chunk)
     span = max_chunks * chunk
@@ -427,12 +430,14 @@
         functools.partial(layer_kernel, (cells_deep, cells_tall), max_chunks, layer),
         grid=(total_cells,),
         out_shape=(
-            jax.ShapeDtypeStruct((total_cells, slots, 4 * width), jnp.bfloat16),
+            jax.ShapeDtypeStruct((total_cells, 1, slots, width), jnp.bfloat16),
+            jax.ShapeDtypeStruct((total_cells, 3, slots, width), jnp.bfloat16),
             jax.ShapeDtypeStruct((8, 128), jnp.float32),
         ),
-        in_specs=[pl.BlockSpec(memory_space=pltpu.SMEM)] + [vmem] * (2 + len(params)),
+        in_specs=[pl.BlockSpec(memory_space=pltpu.SMEM)] + [vmem] * (3 + len(params)),
         out_specs=(
-            pl.BlockSpec((1, slots, 4 * width), lambda i: (i, 0, 0)),
+            pl.BlockSpec((1, 1, slots, width), lambda i: (i, 0, 0, 0)),
+            pl.BlockSpec((1, 3, slots, width), lambda i: (i, 0, 0, 0)),
             pl.BlockSpec((8, 128), lambda i: (0, 0)),
         ),
         scratch_shapes=[
@@ -446,7 +451,7 @@
         ],
         compiler_params=pltpu.CompilerParams(vmem_limit_bytes=56 << 20),
         name="message_layer",
-    )(counts, places, feats, *params)
+    )(counts, places, *states, *params)
 
 
 def on_device(
@@ -468,24 +473,21 @@
     level = jnp.broadcast_to(counts.astype(jnp.float32)[..., None, None], cells_shape + (1, slots))
     geometry = jnp.concatenate([positions, level], axis=3)
     geometry = jnp.pad(geometry, ((0, 0),) * 3 + ((0, 8 - geometry.shape[3]), (0, 128 - slots)))
-    state = jnp.concatenate(
-        [scalars, vectors.reshape(cells_shape + (slots, 3 * width))], axis=-1
-    )
+    geometry = geometry[:, :, :, None]
+    states = [scalars[:, :, :, None], vectors.transpose(0, 1, 2, 4, 3, 5)]
     params = (radial_out, atom_in, atom_bias, atom_out, readout_in.T, readout_out[None, :])
     for layer in range(radial_in.shape[0]):
         if layer == 0:
-            feats, places, near_counts, blocks, bias_wide = extended(
-                state, 0, (geometry, radial_in, radial_bias)
+            *states, places, near_counts, blocks, bias_wide = extended(
+                states, 0, (geometry, radial_in, radial_bias)
             )
             params = (blocks, bias_wide) + params
         else:
-            (feats,) = extended(state, layer)
-        state, part = layer_update(
-            layer, cells_shape, near_counts, places, feats.reshape(-1, slots, 4 * width), params
-        )
-        state = state.reshape(cells_shape + (slots, 4 * width))
-    scalar_state = state[..., :width]
-    vector_state = state[..., width:].reshape(cells_shape + (slots, 3, width))
+            states = extended(states, layer)
+        *states, part = layer_update(layer, cells_shape, near_counts, places, states, params)
+        states = [state.reshape(cells_shape + state.shape[1:]) for state in states]
+    scalar_state = states[0][:, :, :, 0]
+    vector_state = states[1].transpose(0, 1, 2, 4, 3, 5)
     energy = summed(part, ("gz", "gx", "gy"), radial_in.shape[0])
     return (scalar_state, vector_state, energy)
 

time: 94.7 us -> 86.8 us (0.917)
  local copies, waits for them, and re-layouts: 4.42 us -> 0.72 us
  Pallas kernels: 84.5 us -> 82.1 us
  other arithmetic: 2.62 us -> 0.61 us
    pallas_call x2, Pallas kernels: 47.8 us -> 44 us  [extended(): pl.pallas_call(functools.partial(halo_kernel, bool(extra)), out_shape=sha...]
    pallas_call x2, Pallas kernels: 15.9 us -> 18.9 us  [layer_update(): pl.pallas_call(functools.partial(layer_kernel, (cells_deep, cells_tall),...]
    unnamed x4 -> x5, local copies, waits for them, and re-layouts: 3.47 us -> 0.64 us
    concatenate x2 -> x0, other arithmetic: 1.96 us -> none  [the longest x1 1.35 us: on_device(): jnp.concatenate([scalars, vectors.reshape(cells_shape + (slots, 3 * width...]
    pallas_call x1, Pallas kernels: 20.8 us -> 19.3 us  [summed(): pl.pallas_call(functools.partial(total_kernel, axes), out_shape=jax.Shape...]
where the time goes in v4:
time: 86.8 us; the launch traced here: 85.8 us
  Pallas kernels  82.1 us (95%)
  between operations  2.36 us (3%)
    pallas_call x2, Pallas kernels, extended(): pl.pallas_call(functools.partial(halo_kernel, bool(extra)), out_shape=sha...  44 us
    pallas_call x1, Pallas kernels, summed(): pl.pallas_call(functools.partial(total_kernel, axes), out_shape=jax.Shape...  19.3 us
    pallas_call x2, Pallas kernels, layer_update(): pl.pallas_call(functools.partial(layer_kernel, (cells_deep, cells_tall),...  18.9 us

profile of v4, /device:TPU:0, one launch (start us, length us, event | category | flops | bytes accessed | tf_op | source)
XLA Modules:
  0.0 85.8 jit_solution(2621066611972880871)
XLA Ops:
  0.6 0.0 copy-start.1
  0.6 0.0 copy-start
  0.6 0.6 copy-done.1
  1.3 0.1 broadcast_in_dim.19
  1.4 0.0 copy-done
  1.4 0.6 fusion.refs_2_
  2.0 21.7 %halo.2 = (bf16[4,3,3,1,32,128]{5,4,3,2,1,0:T(8,128)(2,1)}, bf16[4,3,3,3,32,128]{5,4,3,2,1,0:T(8,128)(2,1)}, f32[36,32,128]{2,1,0:T(8,128)}, s32[36,128]{1,0:T(8...) custom-call(bf16[2,1,1,1,32,128]{5,4,3,2,1,0:T(8,128)(2,1)} %bitcast.30, ...), custom_call_target="tpu_custom_call" | custom-call | tf_op jit(solution)/shard_map/halo/pallas_call | solution.py:147
  23.7 9.1 %message_layer.2 = (bf16[2,1,32,128]{3,2,1,0:T(8,128)(2,1)}, bf16[2,3,32,128]{3,2,1,0:T(8,128)(2,1)}, f32[8,128]{1,0:T(8,128)}) custom-call(s32[36,128]{1,0:T(8,128)} %get-tuple-element.16.counts, f32[36,32,128]{2,1,0:T(8,128)} %get-tuple-element.17.places, bf16[36,1,32,128]{3,2,1,0:T(8,128)(2,1)} %bitcast.25, bf16[36,3,32,128]{3,2,1,0:T(8,128)(2,1)} %bitcast.23, ...), custom_call_target="tpu_custom_call" | custom-call | tf_op jit(solution)/shard_map/message_layer/pallas_call | solution.py:429
  32.8 22.3 %halo.3 = (bf16[4,3,3,1,32,128]{5,4,3,2,1,0:T(8,128)(2,1)}, bf16[4,3,3,3,32,128]{5,4,3,2,1,0:T(8,128)(2,1)}) custom-call(bf16[2,1,1,1,32,128]{5,4,3,2,1,0:T(8,128)(2,1)} %bitcast.31, bf16[2,1,1,3,32,128]{5,4,3,2,1,0:T(8,128)(2,1)} %bitcast.29), custom_call_target="tpu_custom_call" | custom-call | tf_op jit(solution)/shard_map/halo/pallas_call | solution.py:147
  55.0 9.8 %message_layer.3 = (bf16[2,1,32,128]{3,2,1,0:T(8,128)(2,1)}, bf16[2,3,32,128]{3,2,1,0:T(8,128)(2,1)}, f32[8,128]{1,0:T(8,128)}) custom-call(s32[36,128]{1,0:T(8,128)} %get-tuple-element.16.counts, f32[36,32,128]{2,1,0:T(8,128)} %get-tuple-element.17.places, bf16[36,1,32,128]{3,2,1,0:T(8,128)(2,1)} %bitcast.24, bf16[36,3,32,128]{3,2,1,0:T(8,128)(2,1)} %bitcast.22, ...), custom_call_target="tpu_custom_call" | custom-call | tf_op jit(solution)/shard_map/message_layer/pallas_call | solution.py:429
  64.8 19.3 %total.1 = f32[1]{0:T(128)} custom-call(f32[8,128]{1,0:T(8,128)} %get-tuple-element.28.part), custom_call_target="tpu_custom_call" | custom-call | tf_op jit(solution)/shard_map/total/pallas_call | solution.py:205
  (2 shorter events, 0.0 us)
Async XLA Ops:
  0.6 0.7 copy-start.1
  0.6 0.7 copy-start
